TPU v7x, 32 devices: a whole 2x2x4 slice. The times are simulated.
32 devices in a mesh: member: 2 (over core), dp: 16 (over z, y, x).
Axes of the slice: x: 2, y: 2, z: 4, core: 2. Of those that a mesh axis runs over, the one named last changes fastest.
Arguments:
- features: float32 [4, 256, 16, 256], P('member', 'dp'), may hold values from -6 to 6
- actions: int32 [4, 256, 16], P('member', 'dp'), may hold values from 0 to 127
- advantages: float32 [4, 256, 16], P('member', 'dp'), may hold values from -6 to 6
- h_start: float32 [4, 256, 256], P('member', 'dp'), may hold values from -0.9 to 0.9
- c_start: float32 [4, 256, 256], P('member', 'dp'), may hold values from -4 to 4
- w_lstm: float32 [4, 512, 1024], P('member'), may hold values from -0.25 to 0.25
- b_lstm: float32 [4, 1024], P('member'), may hold values from -3 to 3
- w_head: float32 [4, 256, 128], P('member'), may hold values from -1.875 to 1.875
- head_bias: float32 [4, 128], P('member'), may hold values from -3 to 330
- m_lstm: float32 [4, 512, 1024], P('member', 'dp'), may hold values from -0.06 to 0.06
- m_bias: float32 [4, 1024], P('member', 'dp'), may hold values from -0.06 to 0.06
- m_head: float32 [4, 256, 128], P('member', 'dp'), may hold values from -0.06 to 0.06
- m_head_bias: float32 [4, 128], P('member', 'dp'), may hold values from -0.06 to 0.06
- v_lstm: float32 [4, 512, 1024], P('member', 'dp'), may hold values from 1e-05 to 0.001
- v_bias: float32 [4, 1024], P('member', 'dp'), may hold values from 1e-05 to 0.001
- v_head: float32 [4, 256, 128], P('member', 'dp'), may hold values from 1e-05 to 0.001
- v_head_bias: float32 [4, 128], P('member', 'dp'), may hold values from 1e-05 to 0.001
- winners: int32 [4], replicated, may hold values from 0 to 3
- exploit_flags: int32 [4], replicated, may hold values 0 or 1
Outputs:
- new_w_lstm: float32 [4, 512, 1024], P('member')
- new_b_lstm: float32 [4, 1024], P('member')
- new_w_head: float32 [4, 256, 128], P('member')
- new_head_bias: float32 [4, 128], P('member')
- new_m_lstm: float32 [4, 512, 1024], P('member', 'dp')
- new_m_bias: float32 [4, 1024], P('member', 'dp')
- new_m_head: float32 [4, 256, 128], P('member', 'dp')
- new_m_head_bias: float32 [4, 128], P('member', 'dp')
- new_v_lstm: float32 [4, 512, 1024], P('member', 'dp')
- new_v_bias: float32 [4, 1024], P('member', 'dp')
- new_v_head: float32 [4, 256, 128], P('member', 'dp')
- new_v_head_bias: float32 [4, 128], P('member', 'dp')
All inputs are finite; a program needn't handle non-finite values.
Results may differ from a plain program's by a relative error of at most 0.0003.
Values sent between devices are 32-bit elements; how exact they have to be, the bound alone decides.
No kernel may reach another device: no remote copies, remote signals or barrier semaphores. Data moves between devices by JAX's collectives and lax.ppermute only.
A program may use at most 64 MiB of HBM per device.

v0:
```python
import jax
import jax.numpy as jnp
from jax import lax
from jax.sharding import PartitionSpec as P

B_DEV = 16
TSTEPS = 16


def agent_loss(w_lstm, b_lstm, w_head, head_bias, features, actions, advantages, h_start, c_start):
    hidden = w_head.shape[0]

    def advance(carry, inputs):
        h_state, c_state = carry
        frame, acted, weight = inputs
        joined = jnp.concatenate([frame, h_state], axis=1)
        gates = jnp.dot(joined, w_lstm, precision=lax.Precision.HIGHEST) + b_lstm
        in_gate = jax.nn.sigmoid(gates[:, 0:hidden])
        forget = jax.nn.sigmoid(gates[:, hidden : 2 * hidden])
        cell_in = jnp.tanh(gates[:, 2 * hidden : 3 * hidden])
        out_gate = jax.nn.sigmoid(gates[:, 3 * hidden :])
        c_state = forget * c_state + in_gate * cell_in
        h_state = out_gate * jnp.tanh(c_state)
        logits = jnp.dot(h_state, w_head, precision=lax.Precision.HIGHEST) + head_bias
        top = jnp.max(logits, axis=1, keepdims=True)
        total = jnp.log(jnp.sum(jnp.exp(logits - top), axis=1)) + top[:, 0]
        picked = jnp.sum(
            jnp.where(jnp.arange(logits.shape[1])[None, :] == acted[:, None], logits, 0.0), axis=1
        )
        return ((h_state, c_state), jnp.sum(weight * (total - picked)))

    frames = jnp.transpose(features, (1, 0, 2))
    acts = jnp.transpose(actions, (1, 0))
    weights = jnp.transpose(advantages, (1, 0))
    carry, terms = lax.scan(advance, (h_start, c_start), (frames, acts, weights))
    return jnp.sum(terms) / (B_DEV * TSTEPS)


def adam_update(param, first, second, grad):
    first = 0.9 * first + 0.1 * grad
    second = 0.999 * second + 0.001 * grad * grad
    param = param - 0.01 * first / (jnp.sqrt(second) + 1e-08)
    return (param, first, second)


def local_grads(params, features, actions, advantages, h_start, c_start):
    grad_fn = jax.vmap(jax.grad(agent_loss, argnums=(0, 1, 2, 3)))
    return grad_fn(
        params[0], params[1], params[2], params[3], features, actions, advantages, h_start, c_start
    )


def own_rows(whole, position, count):
    return lax.dynamic_slice_in_dim(whole, position * count, count, 1)


def local(
    features,
    actions,
    advantages,
    h_start,
    c_start,
    w_lstm,
    b_lstm,
    w_head,
    head_bias,
    m_lstm,
    m_bias,
    m_head,
    m_head_bias,
    v_lstm,
    v_bias,
    v_head,
    v_head_bias,
    winners,
    exploit_flags,
):
    params = [w_lstm, b_lstm, w_head, head_bias]
    firsts = [m_lstm, m_bias, m_head, m_head_bias]
    seconds = [v_lstm, v_bias, v_head, v_head_bias]
    counts = [m_lstm.shape[1], m_bias.shape[1], m_head.shape[1], m_head_bias.shape[1]]
    position = lax.axis_index("dp")
    grads = local_grads(params, features, actions, advantages, h_start, c_start)
    shares = (
        lax.psum_scatter(grads[0], "dp", scatter_dimension=1, tiled=True),
        lax.psum_scatter(grads[1], "dp", scatter_dimension=1, tiled=True),
        lax.psum_scatter(grads[2], "dp", scatter_dimension=1, tiled=True),
        lax.psum_scatter(grads[3], "dp", scatter_dimension=1, tiled=True),
    )
    rows = [own_rows(params[k], position, counts[k]) for k in range(4)]
    for k in range(4):
        rows[k], firsts[k], seconds[k] = adam_update(rows[k], firsts[k], seconds[k], shares[k])
    fresh = (
        lax.all_gather(rows[0], "dp", axis=1, tiled=True),
        lax.all_gather(rows[1], "dp", axis=1, tiled=True),
        lax.all_gather(rows[2], "dp", axis=1, tiled=True),
        lax.all_gather(rows[3], "dp", axis=1, tiled=True),
    )
    params = [fresh[0], fresh[1], fresh[2], fresh[3]]
    grads = local_grads(params, features, actions, advantages, h_start, c_start)
    shares = (
        lax.psum_scatter(grads[0], "dp", scatter_dimension=1, tiled=True),
        lax.psum_scatter(grads[1], "dp", scatter_dimension=1, tiled=True),
        lax.psum_scatter(grads[2], "dp", scatter_dimension=1, tiled=True),
        lax.psum_scatter(grads[3], "dp", scatter_dimension=1, tiled=True),
    )
    rows = [own_rows(params[k], position, counts[k]) for k in range(4)]
    for k in range(4):
        rows[k], firsts[k], seconds[k] = adam_update(rows[k], firsts[k], seconds[k], shares[k])
    states = rows + firsts + seconds
    local_count = m_lstm.shape[0]
    mine = lax.axis_index("member") * local_count + jnp.arange(local_count, dtype=jnp.int32)
    flags_mine = jnp.take(exploit_flags, mine, axis=0)
    winners_mine = jnp.take(winners, mine, axis=0)
    source = jnp.where(flags_mine == 1, winners_mine, mine)
    everyone = (
        lax.all_gather(states[0], "member", axis=0, tiled=True),
        lax.all_gather(states[1], "member", axis=0, tiled=True),
        lax.all_gather(states[2], "member", axis=0, tiled=True),
        lax.all_gather(states[3], "member", axis=0, tiled=True),
        lax.all_gather(states[4], "member", axis=0, tiled=True),
        lax.all_gather(states[5], "member", axis=0, tiled=True),
        lax.all_gather(states[6], "member", axis=0, tiled=True),
        lax.all_gather(states[7], "member", axis=0, tiled=True),
        lax.all_gather(states[8], "member", axis=0, tiled=True),
        lax.all_gather(states[9], "member", axis=0, tiled=True),
        lax.all_gather(states[10], "member", axis=0, tiled=True),
        lax.all_gather(states[11], "member", axis=0, tiled=True),
    )
    result = [jnp.take(x, source, axis=0) for x in everyone]
    final = (
        lax.all_gather(result[0], "dp", axis=1, tiled=True),
        lax.all_gather(result[1], "dp", axis=1, tiled=True),
        lax.all_gather(result[2], "dp", axis=1, tiled=True),
        lax.all_gather(result[3], "dp", axis=1, tiled=True),
    )
    return (
        final[0],
        final[1],
        final[2],
        final[3],
        result[4],
        result[5],
        result[6],
        result[7],
        result[8],
        result[9],
        result[10],
        result[11],
    )


def solution(mesh):
    placed = (
        P("member", "dp", None, None),
        P("member", "dp", None),
        P("member", "dp", None),
        P("member", "dp", None),
        P("member", "dp", None),
        P("member", None, None),
        P("member", None),
        P("member", None, None),
        P("member", None),
        P("member", "dp", None),
        P("member", "dp"),
        P("member", "dp", None),
        P("member", "dp"),
        P("member", "dp", None),
        P("member", "dp"),
        P("member", "dp", None),
        P("member", "dp"),
        P(),
        P(),
    )
    return jax.shard_map(
        local,
        mesh=mesh,
        in_specs=placed,
        out_specs=(
            P("member", None, None),
            P("member", None),
            P("member", None, None),
            P("member", None),
            P("member", "dp", None),
            P("member", "dp"),
            P("member", "dp", None),
            P("member", "dp"),
            P("member", "dp", None),
            P("member", "dp"),
            P("member", "dp", None),
            P("member", "dp"),
        ),
        check_vma=False,
    )
```

profile of v0, /device:TPU:0, one launch (start us, length us, event | category | flops | bytes accessed | tf_op | source)
XLA Modules:
  0.0 1384.9 jit_solution(13637193912129934475)
XLA Ops:
  21.5 121.4 %while.148 = (s32[]{:T(128)}, f32[2,16,256]{2,1,0:T(8,128)S(1)}, f32[2,16,256]{2,1,0:T(8,128)S(1)}, f32[16,2,16,512]{3,2,1,0:T(8,128)S(1)}, f32[16,2,16,256]{3,2...) while((s32[]{:T(128)}, f32[2,16,256]{2,1,0:T(8,128)S(1)}, ...), condition=%wide.region_4.5_spmd.clone, body=%wide.region_0.4_spmd.clone.sunk | while | flops 214269856 | bytes 5747849 | solution.py:35
  143.0 221.7 %while.150 = (s32[]{:T(128)}, f32[2,512,1024]{2,1,0:T(8,128)}, f32[2,1024]{1,0:T(2,128)S(1)}, f32[2,256,128]{2,1,0:T(8,128)S(1)}, f32[2,128]{1,0:T(2,128)S(1)}, ...) while((s32[]{:T(128)}, f32[2,512,1024]{2,1,0:T(8,128)}, ...), condition=%wide.region_9.10_spmd.clone, body=%wide.region_5.9_spmd.clone.sunk | while | flops 329861568 | bytes 29370340 | solution.py:35
  366.8 96.1 %reduce-scatter.13.cloned.1.call-done = f32[2,32,1024]{2,1,0:T(8,128)} async-done(((f32[2,512,1024]{2,1,0:T(8,128)}), f32[2,32,1024]{2,1,0:T(8,128)}) %reduce-scatter.13.cloned.1.call-update) | async-done | bytes 262160 | tf_op jit(solution)/shard_map/reduce_scatter | solution.py:85
  466.1 40.1 %all-reduce.8 = f32[2,128]{1,0:T(2,128)S(1)} all-reduce(f32[2,128]{1,0:T(2,128)S(1)} %get-tuple-element.1442), channel_id=5, replica_groups=mesh['member'=2,'dp'=16] {'dp'}, use_global_device_ids=true, to_apply=%region_13.14.clone | all-reduce | flops 256 | bytes 2048
  506.3 35.5 %all-gather.1 = f32[16,8,2]{1,2,0:T(2,128)S(1)} all-gather(f32[1,8,2]{1,2,0:T(2,128)S(1)} %fusion.97), channel_id=1, replica_groups=mesh['member'=2,'dp'=16] {'dp'}, dimensions={0}, use_global_device_ids=true | all-gather | bytes 1088 | tf_op jit(solution)/shard_map/all_gather | solution.py:97
  542.8 37.5 %all-gather = f32[16,64,2]{1,2,0:T(2,128)S(1)} all-gather(f32[1,64,2]{1,2,0:T(2,128)S(1)} %fusion.95), channel_id=1, replica_groups=mesh['member'=2,'dp'=16] {'dp'}, dimensions={0}, use_global_device_ids=true | all-gather | bytes 8704 | tf_op jit(solution)/shard_map/all_gather | solution.py:95
  580.4 36.4 %reduce-scatter.15.cloned.1.call-done = f32[2,16,128]{2,1,0:T(8,128)} async-done(((f32[2,256,128]{2,1,0:T(8,128)}), f32[2,16,128]{2,1,0:T(8,128)}) %reduce-scatter.15.cloned.1.call-update) | async-done | bytes 16400 | tf_op jit(solution)/shard_map/reduce_scatter | solution.py:87
  617.5 38.2 %all_gather.62 = f32[2,256,128]{2,1,0:T(8,128)S(1)} all-gather(f32[2,16,128]{2,1,0:T(8,128)S(1)} %divide_subtract_fusion.3), channel_id=1, replica_groups=mesh['member'=2,'dp'=16] {'dp'}, dimensions={1}, use_global_device_ids=true | all-gather | bytes 278528 | tf_op jit(solution)/shard_map/all_gather | solution.py:96
  655.7 37.5 %all-gather.13.cloned.1.call-done = f32[2,512,1024]{2,1,0:T(8,128)} async-done(((f32[2,32,1024]{2,1,0:T(8,128)}), f32[2,512,1024]{2,1,0:T(8,128)}) %all-gather.13.cloned.1.call-update) | async-done | bytes 4194320 | tf_op jit(solution)/shard_map/all_gather | solution.py:94
  704.6 121.3 %while.149 = (s32[]{:T(128)}, f32[2,16,256]{2,1,0:T(8,128)S(1)}, f32[2,16,256]{2,1,0:T(8,128)S(1)}, f32[16,2,16,512]{3,2,1,0:T(8,128)S(1)}, f32[16,2,16,256]{3,2...) while((s32[]{:T(128)}, f32[2,16,256]{2,1,0:T(8,128)S(1)}, ...), condition=%wide.region_18.19_spmd.clone, body=%wide.region_14.18_spmd.clone.sunk | while | flops 214269856 | bytes 5747849 | solution.py:35
  825.9 222.0 %while.151 = (s32[]{:T(128)}, f32[2,512,1024]{2,1,0:T(8,128)}, f32[2,1024]{1,0:T(2,128)S(1)}, f32[2,256,128]{2,1,0:T(8,128)S(1)}, f32[2,128]{1,0:T(2,128)S(1)}, ...) while((s32[]{:T(128)}, f32[2,512,1024]{2,1,0:T(8,128)}, ...), condition=%wide.region_23.24_spmd.clone, body=%wide.region_19.23_spmd.clone.sunk | while | flops 329861568 | bytes 29370340 | solution.py:35
  869.9 6.9 select_add_fusion.15
  897.8 6.9 select_add_fusion.15
  925.8 6.9 select_add_fusion.15
  953.8 6.9 select_add_fusion.15
  981.7 6.9 select_add_fusion.15
  1009.7 6.9 select_add_fusion.15
  1051.2 90.6 %reduce-scatter.17.cloned.1.call-done = f32[2,32,1024]{2,1,0:T(8,128)} async-done(((f32[2,512,1024]{2,1,0:T(8,128)}), f32[2,32,1024]{2,1,0:T(8,128)}) %reduce-scatter.17.cloned.1.call-update) | async-done | bytes 262160 | tf_op jit(solution)/shard_map/reduce_scatter | solution.py:102
  1152.3 40.1 %all-reduce.9 = f32[2,128]{1,0:T(2,128)S(1)} all-reduce(f32[2,128]{1,0:T(2,128)S(1)} %get-tuple-element.1464), channel_id=9, replica_groups=mesh['member'=2,'dp'=16] {'dp'}, use_global_device_ids=true, to_apply=%region_27.32.clone | all-reduce | flops 256 | bytes 2048
  1200.2 35.5 %all-gather.5 = f32[16,8,2]{1,2,0:T(2,128)S(1)} all-gather(f32[1,8,2]{1,2,0:T(2,128)S(1)} %get-tuple-element.2055), channel_id=1, replica_groups=mesh['member'=2,'dp'=16] {'dp'}, dimensions={0}, use_global_device_ids=true | all-gather | bytes 1088 | tf_op jit(solution)/shard_map/all_gather | solution.py:135
  1244.9 37.5 %all-gather.3 = f32[16,64,2]{1,2,0:T(2,128)S(1)} all-gather(f32[1,64,2]{1,2,0:T(2,128)S(1)} %get-tuple-element.2061), channel_id=1, replica_groups=mesh['member'=2,'dp'=16] {'dp'}, dimensions={0}, use_global_device_ids=true | all-gather | bytes 8704 | tf_op jit(solution)/shard_map/all_gather | solution.py:133
  1283.0 12.1 reduce-scatter.19.cloned.1.call-done
  1303.7 38.4 %all_gather.69 = f32[2,256,128]{2,1,0:T(8,128)S(1)} all-gather(f32[2,16,128]{2,1,0:T(8,128)S(1)} %get-tuple-element.2058), channel_id=1, replica_groups=mesh['member'=2,'dp'=16] {'dp'}, dimensions={1}, use_global_device_ids=true | all-gather | bytes 278528 | tf_op jit(solution)/shard_map/all_gather | solution.py:134
  1342.1 30.4 %all-gather.15.cloned.1.call-done = f32[2,512,1024]{2,1,0:T(8,128)} async-done(((f32[2,32,1024]{2,1,0:T(8,128)}), f32[2,512,1024]{2,1,0:T(8,128)}) %all-gather.15.cloned.1.call-update) | async-done | bytes 4194320 | tf_op jit(solution)/shard_map/all_gather | solution.py:132
  (994 shorter events, 719.8 us)
Async XLA Ops:
  7.2 1040.8 %copy-start = (s32[4]{0:T(128)S(1)}, s32[4]{0:T(128)}, u32[]{:S(2)}) copy-start(s32[4]{0:T(128)} %param.55) | copy-start | bytes 52
  7.2 455.6 %reduce-scatter.13.cloned.1.call-start = ((), (), s32[]{:S(2)}) async-start(), calls=%async_computation.6 | async-start | bytes 4456448 | tf_op jit(solution)/shard_map/reduce_scatter | solution.py:85
  10.1 11.3 copy-start.4
  10.1 11.3 copy-start.10
  10.1 11.3 copy-start.14
  21.5 121.5 %copy-start.15 = (f32[2,16,16]{2,1,0:T(8,128)S(1)}, f32[2,16,16]{2,1,0:T(8,128)}, u32[]{:S(2)}) copy-start(f32[2,16,16]{2,1,0:T(8,128)} %param.39) | copy-start | bytes 6148
  364.7 98.1 %copy-start.7 = (f32[2,32,1024]{2,1,0:T(8,128)S(1)}, f32[2,32,1024]{2,1,0:T(8,128)}, u32[]{:S(2)}) copy-start(f32[2,32,1024]{2,1,0:T(8,128)} %param.46) | copy-start | bytes 786436
  364.7 98.1 %copy-start.8 = (f32[2,32,1024]{2,1,0:T(8,128)S(1)}, f32[2,32,1024]{2,1,0:T(8,128)}, u32[]{:S(2)}) copy-start(f32[2,32,1024]{2,1,0:T(8,128)} %param.50) | copy-start | bytes 786436
  364.7 100.1 %copy-start.20 = (u32[32]{0:T(128)S(1)}, u32[32]{0:T(128)}, u32[]{:S(2)}) copy-start(u32[32]{0:T(128)} %constant.355) | copy-start | bytes 388
  364.8 141.4 %copy-start.16 = (f32[2,8]{1,0:T(2,128)S(1)}, f32[2,8]{1,0:T(2,128)}, u32[]{:S(2)}) copy-start(f32[2,8]{1,0:T(2,128)} %param.49) | copy-start | bytes 196
  364.8 141.4 %copy-start.17 = (f32[2,8]{1,0:T(2,128)S(1)}, f32[2,8]{1,0:T(2,128)}, u32[]{:S(2)}) copy-start(f32[2,8]{1,0:T(2,128)} %param.53) | copy-start | bytes 196
  364.8 178.0 %copy-start.18 = (f32[2,64]{1,0:T(2,128)S(1)}, f32[2,64]{1,0:T(2,128)}, u32[]{:S(2)}) copy-start(f32[2,64]{1,0:T(2,128)} %param.47) | copy-start | bytes 1540
  364.8 177.9 %copy-start.19 = (f32[2,64]{1,0:T(2,128)S(1)}, f32[2,64]{1,0:T(2,128)}, u32[]{:S(2)}) copy-start(f32[2,64]{1,0:T(2,128)} %param.51) | copy-start | bytes 1540
  364.8 252.0 %copy-start.11 = (f32[2,16,128]{2,1,0:T(8,128)S(1)}, f32[2,16,128]{2,1,0:T(8,128)}, u32[]{:S(2)}) copy-start(f32[2,16,128]{2,1,0:T(8,128)} %param.48) | copy-start | bytes 49156
  364.8 252.0 %copy-start.12 = (f32[2,16,128]{2,1,0:T(8,128)S(1)}, f32[2,16,128]{2,1,0:T(8,128)}, u32[]{:S(2)}) copy-start(f32[2,16,128]{2,1,0:T(8,128)} %param.52) | copy-start | bytes 49156
  364.9 177.0 %reduce-scatter.21.cloned.1.call-start = ((), (), s32[]{:S(2)}) async-start(), calls=%async_computation.12 | async-start | bytes 557056
  366.0 250.8 %reduce-scatter.15.cloned.1.call-start = ((), (), s32[]{:S(2)}) async-start(), calls=%async_computation.8 | async-start | bytes 278528 | tf_op jit(solution)/shard_map/reduce_scatter | solution.py:87
  366.7 326.5 %all-gather.13.cloned.1.call-start = ((), (), s32[]{:S(2)}) async-start(), calls=%async_computation.7 | async-start | bytes 4456448 | tf_op jit(solution)/shard_map/all_gather | solution.py:94
  464.8 677.0 %reduce-scatter.17.cloned.1.call-start = ((), (), s32[]{:S(2)}) async-start(), calls=%async_computation.9 | async-start | bytes 4456448 | tf_op jit(solution)/shard_map/reduce_scatter | solution.py:102
  1047.9 93.9 %copy-start.9 = (f32[2,32,1024]{2,1,0:T(8,128)S(1)}, f32[2,32,1024]{2,1,0:T(8,128)}, u32[]{:S(2)}) copy-start(f32[2,32,1024]{2,1,0:T(8,128)} %reduce-scatter.13.cloned.1.call-done) | copy-start | bytes 786436
  1047.9 188.4 %reduce-scatter.23.cloned.1.call-start = ((), (), s32[]{:S(2)}) async-start(), calls=%async_computation.13 | async-start | bytes 557056
  1050.4 244.7 %reduce-scatter.19.cloned.1.call-start = ((), (), s32[]{:S(2)}) async-start(), calls=%async_computation.11 | async-start | bytes 278528 | tf_op jit(solution)/shard_map/reduce_scatter | solution.py:104
  1050.4 244.7 %copy-start.13 = (f32[2,16,128]{2,1,0:T(8,128)S(1)}, f32[2,16,128]{2,1,0:T(8,128)}, u32[]{:S(2)}) copy-start(f32[2,16,128]{2,1,0:T(8,128)} %reduce-scatter.15.cloned.1.call-done) | copy-start | bytes 49156
  1051.1 321.4 %all-gather.15.cloned.1.call-start = ((), (), s32[]{:S(2)}) async-start(), calls=%async_computation.10 | async-start | bytes 4456448 | tf_op jit(solution)/shard_map/all_gather | solution.py:132
  (35 other events, 222.0 us)
Sparse Core Ops, SparseCore 0:
  365.0 97.8 reduce-scatter.12
  465.1 76.0 reduce-scatter.20
  544.1 72.6 reduce-scatter.14
  620.0 73.2 all-gather.12
  1048.0 93.7 reduce-scatter.16
  1143.9 76.3 reduce-scatter.22
  1222.6 72.4 reduce-scatter.18
  1298.4 74.0 all-gather.14
where the time goes:
time: 1400 us; the launch traced here: 1380 us
  matrix products  504 us (36%)
  blocking collectives  326 us (23%)
  waiting for transfers between devices  304 us (22%)
  other arithmetic  168 us (12%)
  local copies, waits for them, and re-layouts  65.5 us (5%)
  between operations  15.3 us (1%)
    dot_general x96, matrix products, advance(): gates = jnp.dot(joined, w_lstm, precision=lax.Precision.HIGHEST) + b_lstm  412 us
    reduce_scatter x2, waiting for transfers between devices, local(): lax.psum_scatter(grads[0], 'dp', scatter_dimension=1, tiled=True)  187 us
    dot_general x96, matrix products, advance(): jnp.dot(h_state, w_head, precision=lax.Precision.HIGHEST) + head_bias  91.5 us
    unnamed x2, blocking collectives  80.2 us
    dynamic_update_slice x160, other arithmetic, agent_loss(): lax.scan(advance, (h_start, c_start), (frames, acts, weights))  69.3 us
    reduce_scatter x2, waiting for transfers between devices, local(): lax.psum_scatter(grads[2], 'dp', scatter_dimension=1, tiled=True)  48.4 us
    all_gather x1, blocking collectives, local(): lax.all_gather(result[2], 'dp', axis=1, tiled=True)  38.4 us
    all_gather x1, blocking collectives, local(): lax.all_gather(rows[2], 'dp', axis=1, tiled=True)  38.2 us
  transfers between devices with their start and end apart: 8, of which 6 were waited for; matrix products, arithmetic and copies ran while one was open for 2% of the time, Pallas kernels for 0%

commit v1 on v0

v1 whole, which is shorter than its diff:
```python
import functools
import jax
import jax.numpy as jnp
from jax import lax
from jax.experimental import pallas as pl
from jax.experimental.pallas import tpu as pltpu
from jax.sharding import Mesh, PartitionSpec as P

F32 = jnp.float32
BF16 = jnp.bfloat16
LOSS_SCALE = 1.0 / 256.0
QUAD = 4
NN = ((1,), (0,))
NT = ((1,), (1,))
TN = ((0,), (0,))
VMEM_LIMIT = 56 << 20


def split(x):
    hi = x.astype(BF16)
    return hi, (x - hi.astype(F32)).astype(BF16)


def mm(a, b, dims):
    return lax.dot_general(a, b, (dims, ((), ())), preferred_element_type=F32)


def dot3(a, b, dims):
    return mm(a[0], b[0], dims) + (mm(a[1], b[0], dims) + mm(a[0], b[1], dims))


def dot3_few(a, b, dims):
    n = a[0].shape[0]
    r = mm(jnp.concatenate([a[0], a[1]], 0), b[0], dims)
    return r[:n] + (r[n:] + mm(a[0], b[1], dims))


class Sizes:
    def __init__(self, R, rows, wide, hid, act):
        self.R, self.rows, self.wide, self.hid, self.act = R, rows, wide, hid, act
        D = QUAD * R
        self.B = rows // D
        self.half = self.B // 2
        self.W = QUAD * self.half
        self.h = hid // D // 2
        self.CH = self.W + 8
        self.b_each = wide // D
        self.hb_each = act // D
        self.bl = wide // 2


def own_bias(S, r):
    at = lax.broadcasted_iota(jnp.int32, (2, S.bl), 0) * S.bl + lax.broadcasted_iota(jnp.int32, (2, S.bl), 1)
    return ((at // S.b_each) & (S.R - 1)) == r


def own_head_bias(S, r):
    at = lax.broadcasted_iota(jnp.int32, (1, S.act), 1)
    return ((at // S.hb_each) & (S.R - 1)) == r


def grad_kernel(S, T, packed, *refs):
    who, x_ref = refs[0], refs[1]
    n_in = 2 * S.R if packed else 4
    w_in = refs[2 : 2 + n_in]
    keep, send = refs[2 + n_in : 4 + n_in]
    (xs, zx, gi, gf, gg, go, tc, cp, hs, dhh, lgs, dzh, dzl, whi, wlo, ws, whs, bs, hbs) = refs[4 + n_in :]
    c, r = who[0], who[1]
    nb = x_ref.shape[2]
    IN = x_ref.shape[3]
    H = S.hid
    N = QUAD * nb
    rows_all = T * N
    R, B, half, W, h = S.R, S.B, S.half, S.W, S.h

    if packed:
        rel_of = bit_orders(R)
        bias = jnp.zeros((2, S.bl), F32)
        hbias = jnp.zeros((1, S.act), F32)
        for i in range(2 * R):
            mine = i < R
            ref = w_in[i]
            hc = c if mine else 1 - c
            rel = jnp.where(hc == 0, rel_of[0][i % R], rel_of[1][i % R])
            src = r ^ rel
            for z in range(QUAD):
                at = pl.multiple_of((z * R + src) * B + hc * half, half)
                ws[pl.ds(at, half), :] = ref[z * half : (z + 1) * half, :]
                at = pl.multiple_of(((z * R + src) * 2 + hc) * h, h)
                whs[pl.ds(at, h), :] = ref[W : W + h, z * S.act : (z + 1) * S.act]
            bias += jnp.where(hc == 0, ref[W : W + 2, S.bl :], 0.0)
            hbias += jnp.where(hc == 0, ref[W + 2 : W + 3, S.bl : S.bl + S.act], 0.0)
        bs[:, 0 : S.bl] = bias[0:1]
        bs[:, S.bl :] = bias[1:2]
        hbs[...] = hbias
        w_ref, b_ref, wh_ref, hb_ref = ws, bs, whs, hbs
    else:
        w_ref, b_ref, wh_ref, hb_ref = w_in
    hi, lo = split(w_ref[...])
    whi[...] = hi
    wlo[...] = lo

    for z in range(QUAD):
        xs[:, z] = x_ref[z, 0:T]
    xv = split(xs[...].reshape(rows_all, IN))
    zx[...] = dot3(xv, (whi[0:IN], wlo[0:IN]), NN) + b_ref[...]
    h0 = x_ref[:, T].reshape(N, IN)
    c0 = x_ref[:, T + 1].reshape(N, IN)
    aux = x_ref[:, T + 2].reshape(N, IN)

    def forward(t, carry):
        hv, cv = carry
        at = pl.ds(pl.multiple_of(t * N, N), N)
        hs[at, :] = hv
        cp[at, :] = cv
        z = zx[at, :] + dot3_few(split(hv), (whi[IN:], wlo[IN:]), NN)
        i = jax.nn.sigmoid(z[:, 0:H])
        f = jax.nn.sigmoid(z[:, H : 2 * H])
        g = jnp.tanh(z[:, 2 * H : 3 * H])
        o = jax.nn.sigmoid(z[:, 3 * H :])
        cv = f * cv + i * g
        th = jnp.tanh(cv)
        gi[at, :] = i
        gf[at, :] = f
        gg[at, :] = g
        go[at, :] = o
        tc[at, :] = th
        return o * th, cv

    hv, _ = lax.fori_loop(0, T, forward, (h0, c0))
    hs[rows_all : rows_all + N, :] = hv

    hh = split(hs[N : rows_all + N, :])
    whp = split(wh_ref[...])
    lgs[...] = dot3(hh, whp, NN) + hb_ref[...]
    lane = lax.broadcasted_iota(jnp.int32, (N, S.act), 1).astype(F32)
    for t in range(T):
        lg = lgs[t * N : (t + 1) * N, :]
        e = jnp.exp(lg - jnp.max(lg, axis=1, keepdims=True))
        p = e / jnp.sum(e, axis=1, keepdims=True)
        hot = jnp.where(lane == aux[:, T + t : T + t + 1], 1.0, 0.0)
        lgs[t * N : (t + 1) * N, :] = (aux[:, t : t + 1] * LOSS_SCALE) * (p - hot)
    dl = lgs[...]
    d_hb = jnp.sum(dl, axis=0, keepdims=True)
    dls = split(dl)
    d_wh = dot3(hh, dls, TN)
    dhh[...] = dot3(dls, whp, NT)

    def backward(k, carry):
        rec, dc = carry
        t = T - 1 - k
        at = pl.ds(pl.multiple_of(t * N, N), N)
        i, f, g, o, th = gi[at, :], gf[at, :], gg[at, :], go[at, :], tc[at, :]
        dh = dhh[at, :] + rec
        dc = dc + dh * o * (1.0 - th * th)
        dz = jnp.concatenate(
            [
                dc * g * (i * (1.0 - i)),
                dc * cp[at, :] * (f * (1.0 - f)),
                dc * i * (1.0 - g * g),
                dh * th * (o * (1.0 - o)),
            ],
            axis=1,
        )
        zh, zl = split(dz)
        dzh[at, :] = zh
        dzl[at, :] = zl
        zx[at, :] = dz
        return dot3_few((zh, zl), (whi[IN:], wlo[IN:]), NT), dc * f

    zero = jnp.zeros((N, H), F32)
    lax.fori_loop(0, T, backward, (zero, zero))
    d_b = jnp.sum(zx[...], axis=0, keepdims=True)

    first = c == 0
    dz = (dzh[...], dzl[...])
    span = R * B
    for z in range(QUAD):
        lo_row = z * span
        if lo_row < IN:
            left = (xv[0][:, lo_row : lo_row + span], xv[1][:, lo_row : lo_row + span])
        else:
            left = split(hs[0:rows_all, lo_row - IN : lo_row - IN + span])
        dw = dot3(left, dz, TN)
        for rr in range(R):
            a = dw[rr * B : rr * B + half]
            b = dw[rr * B + half : (rr + 1) * B]
            keep[rr, z * half : (z + 1) * half, :] = jnp.where(first, a, b)
            send[rr, z * half : (z + 1) * half, :] = jnp.where(first, b, a)
    d_b2 = jnp.concatenate([d_b[:, 0 : S.bl], d_b[:, S.bl :]], axis=0)
    for rr in range(R):
        for ref in (keep, send):
            ref[rr, W:, :] = jnp.zeros((8, S.wide), F32)
            ref[rr, W : W + 2, S.bl :] = jnp.where(own_bias(S, rr), d_b2, 0.0)
            ref[rr, W + 2 : W + 3, S.bl : S.bl + S.act] = jnp.where(own_head_bias(S, rr), d_hb, 0.0)
        for z in range(QUAD):
            at = (z * R + rr) * 2 * h
            a = d_wh[at : at + h]
            b = d_wh[at + h : at + 2 * h]
            keep[rr, W : W + h, z * S.act : (z + 1) * S.act] = jnp.where(first, a, b)
            send[rr, W : W + h, z * S.act : (z + 1) * S.act] = jnp.where(first, b, a)


def bit_orders(R):
    bits = [1 << s for s in range(R.bit_length() - 1)]
    orders = []
    for order in (bits, bits[::-1]):
        rels = [0]
        for b in order:
            rels += [x ^ b for x in rels]
        orders.append(rels)
    return orders


def grads_call(S, T, packed, who, x, weights):
    nb, IN = x.shape[2], x.shape[3]
    N = QUAD * nb
    rows = T * N
    V = pltpu.VMEM
    chunk = jax.ShapeDtypeStruct((S.R, S.CH, S.wide), F32)
    gate = V((rows, S.hid), F32)
    wide16 = V((rows, S.wide), BF16)
    w16 = V((S.rows, S.wide), BF16)
    n_in = len(weights)
    flops = 2 * rows * S.wide * (S.rows + S.rows + S.hid) * 3
    return pl.pallas_call(
        functools.partial(grad_kernel, S, T, packed),
        out_shape=(chunk, chunk),
        in_specs=[pl.BlockSpec(memory_space=pltpu.SMEM)] + [pl.BlockSpec(memory_space=pltpu.VMEM)] * (1 + n_in),
        out_specs=[pl.BlockSpec(memory_space=pltpu.VMEM)] * 2,
        scratch_shapes=[
            V((T, QUAD, nb, IN), F32),
            V((rows, S.wide), F32),
            gate, gate, gate, gate, gate, gate,
            V((rows + N, S.hid), F32),
            gate,
            V((rows, S.act), F32),
            wide16, wide16, w16, w16,
            V((S.rows, S.wide), F32),
            V((S.hid, S.act), F32),
            V((1, S.wide), F32),
            V((1, S.act), F32),
        ],
        compiler_params=pltpu.CompilerParams(vmem_limit_bytes=VMEM_LIMIT),
        cost_estimate=pl.CostEstimate(flops=flops * 8, transcendentals=rows * S.hid * 5, bytes_accessed=8 << 20),
        name="lstm_grads",
    )(who, x, *weights)


def adam(p, m, v, g):
    m = 0.9 * m + 0.1 * g
    v = 0.999 * v + 0.001 * g * g
    return p - 0.01 * m / (jnp.sqrt(v) + 1e-08), m, v


def total(parts):
    g = parts[0]
    for i in range(1, parts.shape[0]):
        g = g + parts[i]
    return g


def first_adam_kernel(S, who, g_ref, w_ref, b_ref, wh_ref, hb_ref, mv0, mv1, mv2, mv3, p_out, m_out, v_out):
    c, r, q = who[0], who[1], who[2]
    W, half, h, B, R = S.W, S.half, S.h, S.B, S.R
    for ref in (p_out, m_out, v_out):
        ref[W:, :] = jnp.zeros((8, S.wide), F32)
    moments = (mv0, mv1, mv2, mv3)

    def put(at, lanes, new):
        for ref, x in zip((p_out, m_out, v_out), new):
            ref[at, lanes] = x

    every = slice(None)
    mb = jnp.zeros((2, S.bl), F32)
    vb, mhb, vhb = mb, jnp.zeros((1, S.act), F32), jnp.zeros((1, S.act), F32)
    for s in range(QUAD):
        z = (q - s) & (QUAD - 1)
        ref = moments[s]
        at = pl.ds(pl.multiple_of(z * half, half), half)
        g = g_ref[0, at, :]
        for i in range(1, R):
            g = g + g_ref[i, at, :]
        p = w_ref[pl.ds(pl.multiple_of((z * R + r) * B + c * half, half), half), :]
        put(at, every, adam(p, ref[0:half, :], ref[half:B, :], g))
        lanes = pl.ds(pl.multiple_of(z * S.act, S.act), S.act)
        at = slice(W, W + h)
        g = g_ref[0, at, lanes]
        for i in range(1, R):
            g = g + g_ref[i, at, lanes]
        p = wh_ref[pl.ds(pl.multiple_of(((z * R + r) * 2 + c) * h, h), h), :]
        put(at, lanes, adam(p, ref[B : B + h, 0 : S.act], ref[B : B + h, S.act : 2 * S.act], g))
        mb = mb + ref[B : B + 2, S.bl :]
        vb = vb + ref[B + 2 : B + 4, S.bl :]
        mhb = mhb + ref[B + 4 : B + 5, S.bl : S.bl + S.act]
        vhb = vhb + ref[B + 5 : B + 6, S.bl : S.bl + S.act]
    b2 = jnp.concatenate([b_ref[:, 0 : S.bl], b_ref[:, S.bl :]], axis=0)
    p = jnp.where(own_bias(S, r), b2, 0.0)
    put(slice(W, W + 2), slice(S.bl, None), adam(p, mb, vb, total(g_ref[:, W : W + 2, S.bl :])))
    p = jnp.where(own_head_bias(S, r), hb_ref[...], 0.0)
    lanes = slice(S.bl, S.bl + S.act)
    put(slice(W + 2, W + 3), lanes, adam(p, mhb, vhb, total(g_ref[:, W + 2 : W + 3, lanes])))


def second_adam_kernel(S, g_ref, p_ref, m_ref, v_ref, p_out, mv_out):
    W, half, h, B = S.W, S.half, S.h, S.B
    p, m, v = adam(p_ref[...], m_ref[...], v_ref[...], total(g_ref[...]))
    p_out[...] = p
    for z in range(QUAD):
        mv_out[z, 0:half, :] = m[z * half : (z + 1) * half]
        mv_out[z, half:B, :] = v[z * half : (z + 1) * half]
        mv_out[z, B:, :] = jnp.zeros((8, S.wide), F32)
        mv_out[z, B : B + h, 0 : S.act] = m[W : W + h, z * S.act : (z + 1) * S.act]
        mv_out[z, B : B + h, S.act : 2 * S.act] = v[W : W + h, z * S.act : (z + 1) * S.act]
        mv_out[z, B : B + 2, S.bl :] = m[W : W + 2, S.bl :]
        mv_out[z, B + 2 : B + 4, S.bl :] = v[W : W + 2, S.bl :]
        mv_out[z, B + 4 : B + 5, S.bl : S.bl + S.act] = m[W + 2 : W + 3, S.bl : S.bl + S.act]
        mv_out[z, B + 5 : B + 6, S.bl : S.bl + S.act] = v[W + 2 : W + 3, S.bl : S.bl + S.act]


def vmem_call(fn, name, out_shape, smem, *args):
    specs = [pl.BlockSpec(memory_space=pltpu.SMEM)] * smem
    specs += [pl.BlockSpec(memory_space=pltpu.VMEM)] * (len(args) - smem)
    return pl.pallas_call(
        fn,
        out_shape=out_shape,
        in_specs=specs,
        out_specs=jax.tree.map(lambda _: pl.BlockSpec(memory_space=pltpu.VMEM), out_shape),
        compiler_params=pltpu.CompilerParams(vmem_limit_bytes=VMEM_LIMIT),
        name=name,
    )(*args)


def unpack_kernel(S, L, who, *refs):
    c, r = who[0], who[1]
    pieces = refs[: 2 * S.R]
    w_out, b_out, wh_out, hb_out = refs[2 * S.R :]
    R, B, half, W, h = S.R, S.B, S.half, S.W, S.h
    rel_of = bit_orders(R)
    for l in range(L):
        bias = jnp.zeros((2, S.bl), F32)
        hbias = jnp.zeros((1, S.act), F32)
        for i in range(2 * R):
            hc = c if i < R else 1 - c
            src = r ^ jnp.where(c == 0, rel_of[0][i % R], rel_of[1][i % R])
            ref = pieces[i]
            for z in range(QUAD):
                at = pl.multiple_of((z * R + src) * B + hc * half, half)
                w_out[l, pl.ds(at, half), :] = ref[l, z * half : (z + 1) * half, :]
                at = pl.multiple_of(((z * R + src) * 2 + hc) * h, h)
                wh_out[l, pl.ds(at, h), :] = ref[l, W : W + h, z * S.act : (z + 1) * S.act]
            if i < R:
                bias = bias + ref[l, W : W + 2, S.bl :]
                hbias = hbias + ref[l, W + 2 : W + 3, S.bl : S.bl + S.act]
        b_out[l : l + 1, 0 : S.bl] = bias[0:1]
        b_out[l : l + 1, S.bl :] = bias[1:2]
        hb_out[l : l + 1, :] = hbias


def swap_cores(x):
    return lax.ppermute(x, "c", [(0, 1), (1, 0)])


def gather_columns(R, arrays):
    bits = [1 << s for s in range(R.bit_length() - 1)]
    held = [list(arrays)]
    for up, down in zip(bits, bits[::-1]):
        pairs = [(j, j ^ up) for j in range(R)] + [(R + j, R + (j ^ down)) for j in range(R)]
        held += [[lax.ppermute(x, ("c", "r"), pairs) for x in xs] for xs in held]
    return held


def pick(options, index):
    out = options[-1]
    for i in range(len(options) - 2, -1, -1):
        out = jnp.where(index == i, options[i], out)
    return out


def local(K, R, features, actions, advantages, h_start, c_start, w_lstm, b_lstm, w_head, head_bias,
          m_lstm, m_bias, m_head, m_head_bias, v_lstm, v_bias, v_head, v_head_bias, winners, exploit_flags):
    L, n, T, IN = features.shape
    S = Sizes(R, w_lstm.shape[1], w_lstm.shape[2], w_head.shape[1], w_head.shape[2])
    k, c, q, r = (lax.axis_index(a).astype(jnp.int32) for a in "kcqr")
    D = QUAD * R
    d = q * R + r
    who = jnp.stack([c, r, q])

    mine = (q >> 1) == c
    state = (w_lstm, b_lstm.reshape(L, 1, -1), w_head, head_bias.reshape(L, 1, -1))
    ours = [lax.dynamic_index_in_dim(x, q & 1, 0, keepdims=False) for x in state]
    weights = [jnp.where(mine, x, swap_cores(x)) for x in ours]

    aux = jnp.concatenate([advantages, actions.astype(F32)], axis=2)
    aux = jnp.pad(aux, ((0, 0), (0, 0), (0, IN - 2 * T)))
    seq = jnp.concatenate(
        [features.transpose(0, 2, 1, 3), h_start[:, None], c_start[:, None], aux[:, None]], axis=1
    ).reshape(L, T + 3, 2, n // 2, IN)
    here = lax.dynamic_index_in_dim(seq, c, 2, keepdims=False)
    there = swap_cores(lax.dynamic_index_in_dim(seq, 1 - c, 2, keepdims=False))
    x = jnp.concatenate([jnp.where(c == 0, here, there), jnp.where(c == 0, there, here)], axis=0)
    x = lax.all_to_all(x, "q", 0, 0, tiled=True)

    lanes = jnp.arange(S.wide, dtype=jnp.int32)

    def spread(b, each):
        width = b.shape[1] * D
        return jnp.where(lanes[:width] // each == d, jnp.tile(b, (1, D)), 0.0)

    def rest(m, v, mb, vb, mhb, vhb, side):
        heads = jnp.concatenate([lax.dynamic_slice_in_dim(a, side * S.h, S.h, 1) for a in (m, v)], axis=2)
        heads = jnp.pad(heads, ((0, 0), (0, 8 - S.h), (0, S.bl - 2 * S.act)))
        hb = jnp.pad(jnp.stack([spread(mhb, S.hb_each), spread(vhb, S.hb_each)], axis=1), ((0, 0), (0, 2), (0, S.bl - S.act)))
        biases = [spread(a, S.b_each).reshape(L, 2, S.bl) for a in (mb, vb)]
        return jnp.concatenate([heads, jnp.concatenate(biases + [hb], axis=1)], axis=2)

    def moment_block(side):
        rows = [lax.dynamic_slice_in_dim(a, side * S.half, S.half, 1) for a in (m_lstm, v_lstm)]
        extra = rest(m_head, v_head, m_bias, v_bias, m_head_bias, v_head_bias, side)
        return jnp.concatenate(rows + [extra], axis=1)

    here = moment_block(c)
    there = swap_cores(moment_block(1 - c))
    blocks = jnp.concatenate([jnp.where(c == 0, here, there), jnp.where(c == 0, there, here)], axis=0)
    moments = [lax.dynamic_index_in_dim(blocks, q, 0, keepdims=False)]
    for s in range(1, QUAD):
        block = lax.dynamic_index_in_dim(blocks, (q + s) & (QUAD - 1), 0, keepdims=False)
        moments.append(lax.ppermute(block, "q", [(i, (i + s) % QUAD) for i in range(QUAD)]))

    chunk = jax.ShapeDtypeStruct((S.CH, S.wide), F32)

    def reduced(keep, send):
        return lax.all_to_all(keep + swap_cores(send), "r", 0, 0, tiled=True)

    g = reduced(*grads_call(S, T, False, who, x, weights))
    p, m, v = vmem_call(
        functools.partial(first_adam_kernel, S), "first_adam", (chunk, chunk, chunk), 1, who, g, *weights, *moments
    )
    held = [a for [a] in gather_columns(R, [p])]
    held += [swap_cores(a) for a in held]
    g = reduced(*grads_call(S, T, True, who, x, held))
    block = jax.ShapeDtypeStruct((QUAD, S.B + 8, S.wide), F32)
    p, mv = vmem_call(functools.partial(second_adam_kernel, S), "second_adam", (chunk, block), 0, g, p, m, v)

    everyone = jnp.arange(winners.shape[0], dtype=jnp.int32)
    source = jnp.where(exploit_flags == 1, winners, everyone)

    def source_of(side, l):
        a = (2 * k + side) * L + l
        return jnp.sum(jnp.where(everyone == a, source, 0))

    def chosen(by_agent, side):
        return jnp.stack([by_agent(source_of(side, l)) for l in range(L)])

    shifted = [p] + [lax.ppermute(p, "q", [(i, (i + s) % QUAD) for i in range(QUAD)]) for s in range(1, QUAD)]
    if K > 1:
        groups = lax.all_gather(jnp.stack(shifted), "k")

        def weights_of(a):
            return lax.dynamic_index_in_dim(groups.reshape(K * QUAD, S.CH, S.wide), (a >> 2) * QUAD + ((q - a) & 3), 0, keepdims=False)
    else:

        def weights_of(a):
            return pick(shifted, (q - a) & 3)

    here = chosen(weights_of, c)
    there = swap_cores(chosen(weights_of, 1 - c))
    held = gather_columns(R, [here, there])
    pieces = [a for a, _ in held] + [b for _, b in held]

    f = lambda *dims: jax.ShapeDtypeStruct(dims, F32)
    new_w, new_b, new_wh, new_hb = vmem_call(
        functools.partial(unpack_kernel, S, L), "unpack",
        (f(L, S.rows, S.wide), f(L, S.wide), f(L, S.hid, S.act), f(L, S.act)), 1, who, *pieces,
    )

    mv = lax.all_to_all(mv, "q", 0, 0, tiled=True)
    if K > 1:
        mv = lax.all_gather(mv, "k").reshape(K * QUAD, S.B + 8, S.wide)

    def moments_of(a):
        return lax.dynamic_index_in_dim(mv, a, 0, keepdims=False)

    here = chosen(moments_of, c)
    there = swap_cores(chosen(moments_of, 1 - c))
    lo, hi = jnp.where(c == 0, here, there), jnp.where(c == 0, there, here)
    B, half, h = S.B, S.half, S.h
    out = []
    for i in range(2):
        rows = jnp.concatenate([a[:, i * half : (i + 1) * half] for a in (lo, hi)], axis=1)
        bias = lo[:, B + 2 * i : B + 2 * i + 2, S.bl :].reshape(L, S.wide)
        head = jnp.concatenate([a[:, B : B + h, i * S.act : (i + 1) * S.act] for a in (lo, hi)], axis=1)
        hb = lo[:, B + 4 + i, S.bl : S.bl + S.act]
        out += [
            rows,
            lax.dynamic_slice_in_dim(bias, d * S.b_each, S.b_each, 1),
            head,
            lax.dynamic_slice_in_dim(hb, d * S.hb_each, S.hb_each, 1),
        ]
    return (new_w, new_b, new_wh, new_hb, *out)


def solution(mesh):
    M, D = mesh.shape["member"], mesh.shape["dp"]
    K, R = M // 2, D // QUAD
    inner = Mesh(mesh.devices.reshape(K, 2, QUAD, R), ("k", "c", "q", "r"))
    member, dp = ("k", "c"), ("q", "r")
    full = [P(member, None, None), P(member, None), P(member, None, None), P(member, None)]
    rows = [P(member, dp, None), P(member, dp), P(member, dp, None), P(member, dp)]
    seqs = [P(member, dp, None, None)] + [P(member, dp, None)] * 4
    return jax.shard_map(
        functools.partial(local, K, R),
        mesh=inner,
        in_specs=(*seqs, *full, *rows, *rows, P(), P()),
        out_specs=(*full, *rows, *rows),
        check_vma=False,
    )
```

time: 1400 us -> 251 us (0.18)
  matrix products: 504 us -> 0 us
  blocking collectives: 326 us -> 19.3 us
  waiting for transfers between devices: 304 us -> 103 us
  other arithmetic: 168 us -> 15.6 us
  Pallas kernels: 0 us -> 49.7 us
  local copies, waits for them, and re-layouts: 65.5 us -> 16.4 us
  starting transfers between devices: 0.33 us -> 34.2 us
    dot_general x192 -> x0, matrix products: 504 us -> none  [the longest x96 412 us: advance(): gates = jnp.dot(joined, w_lstm, precision=lax.Precision.HIGHEST) + b_lstm]
    all_gather x18 -> x0, blocking collectives: 245 us -> none  [the longest x1 38.4 us: local(): lax.all_gather(result[2], 'dp', axis=1, tiled=True)]
    reduce_scatter x4 -> x0, waiting for transfers between devices: 235 us -> none  [the longest x2 187 us: local(): lax.psum_scatter(grads[0], 'dp', scatter_dimension=1, tiled=True)]
    ppermute x0 -> x29, waiting for transfers between devices: none -> 91.6 us  [the longest x9 37.6 us: gather_columns(): held += [[lax.ppermute(x, ('c', 'r'), pairs) for x in xs] for xs in held]]
    unnamed x2 -> x0, blocking collectives: 80.2 us -> none
    dynamic_update_slice x160 -> x0, other arithmetic: 69.3 us -> none  [agent_loss(): lax.scan(advance, (h_start, c_start), (frames, acts, weights))]
    all_gather x2 -> x0, waiting for transfers between devices: 67.9 us -> none  [the longest x1 37.5 us: local(): lax.all_gather(rows[0], 'dp', axis=1, tiled=True)]
    reduce_sum x128 -> x1, other arithmetic: 61.9 us -> 0.67 us  [source_of(): return jnp.sum(jnp.where(everyone == a, source, 0))]
  transfers between devices with their start and end apart: 8 -> 32, of which waited for: 6 -> 14; matrix products, arithmetic and copies ran while one was open for 2% -> 10% of each run, Pallas kernels for 0% -> 0%
where the time goes in v1:
time: 251 us; the launch traced here: 250 us
  waiting for transfers between devices  103 us (41%)
  Pallas kernels  49.7 us (20%)
  starting transfers between devices  34.2 us (14%)
  blocking collectives  19.3 us (8%)
  local copies, waits for them, and re-layouts  16.4 us (7%)
  other arithmetic  15.6 us (6%)
  between operations  11.5 us (5%)
    pallas_call x2, Pallas kernels, grads_call(): pl.pallas_call(functools.partial(grad_kernel, S, T, packed), out_shape=(c...  39 us
    ppermute x9, waiting for transfers between devices, gather_columns(): held += [[lax.ppermute(x, ('c', 'r'), pairs) for x in xs] for xs in held]  37.6 us
    ppermute x3, waiting for transfers between devices, local(): lax.ppermute(p, 'q', [(i, (i + s) % QUAD) for i in range(QUAD)])  33.5 us
    all_to_all x1, blocking collectives, reduced(): return lax.all_to_all(keep + swap_cores(send), 'r', 0, 0, tiled=True)  19.3 us
    ppermute x3, waiting for transfers between devices, local(): lax.ppermute(block, 'q', [(i, (i + s) % QUAD) for i in range(QUAD)])  13.7 us
    all_to_all x1, waiting for transfers between devices, local(): x = lax.all_to_all(x, 'q', 0, 0, tiled=True)  11.3 us
    pallas_call x3, Pallas kernels, vmem_call(): pl.pallas_call(fn, out_shape=out_shape, in_specs=specs, out_specs=jax.tre...  10.7 us
    ppermute x9, starting transfers between devices, gather_columns(): held += [[lax.ppermute(x, ('c', 'r'), pairs) for x in xs] for xs in held]  9.72 us
  transfers between devices with their start and end apart: 32, of which 14 were waited for; matrix products, arithmetic and copies ran while one was open for 10% of the time, Pallas kernels for 0%

profile of v1, /device:TPU:0, one launch (start us, length us, event | category | flops | bytes accessed | tf_op | source)
XLA Modules:
  0.0 249.8 jit_solution(4042294246348547808)
XLA Ops:
  2.4 3.2 %dynamic-slice_bitcast_fusion = f32[512,1024]{1,0:T(8,128)} fusion(f32[2,512,1024]{2,1,0:T(8,128)} %param.24, s32[]{:T(128)S(6)} %select_n.285), kind=kLoop, calls=%fused_computation | loop fusion | bytes 4194308 | tf_op jit(solution)/shard_map/jit(dynamic_index_in_dim)/squeeze | solution.py:391
  11.3 6.0 %all-to-all-start = ((f32[4,19,8,256]{3,2,1,0:T(8,128)}), f32[4,19,8,256]{3,2,1,0:T(8,128)S(1)}, u32[]{:S(2)}, u32[]{:S(2)}) async-start(f32[4,19,8,256]{3,2,1,0:T(8,128)} %pad_maximum_fusion), calls=%async_computation | async-start | bytes 1245184 | tf_op jit(solution)/shard_map/all_to_all | solution.py:402
  19.8 3.3 %broadcast_select_fusion.refs_2_.w_ref = f32[512,1024]{1,0:T(8,128)} fusion(f32[512,1024]{1,0:T(8,128)S(1)} %collective-permute-done.1, pred[]{:T(512)S(6)} %eq.112, f32[2,512,1024]{2,1,0:T(8,128)} %param.24, s32[]{:T(128)S(6)} %select_n.285), kind=kLoop, calls=%fused_computation.1 | loop fusion | flops 524288 | bytes 6291461 | tf_op jit(solution)/shard_map/jit(_where)/select_n | solution.py:392
  23.1 11.3 %all-to-all-done.refs_1_ = f32[4,19,8,256]{3,2,1,0:T(8,128)S(1)} async-done(((f32[4,19,8,256]{3,2,1,0:T(8,128)}), f32[4,19,8,256]{3,2,1,0:T(8,128)S(1)}, u32[]{:S(2)}, u32[]{:S(2)}) %all-to-all-start) | async-done | bytes 622624 | tf_op jit(solution)/shard_map/all_to_all | solution.py:402
  35.3 19.4 %lstm_grads.2 = (f32[4,72,1024]{2,1,0:T(8,128)}, f32[4,72,1024]{2,1,0:T(8,128)}) custom-call(s32[3]{0:T(128)} %pad_add_fusion.refs_0_.who, f32[4,19,8,256]{3,2,1,0:T(8,128)} %copy-done.4, f32[512,1024]{1,0:T(8,128)} %broadcast_select_fusion.refs_2_.w_ref, f32[1,1024]{1,0:T(1,128)} %broadcast_select_fusion.6.refs_3_.b_ref, ...), custom_call_target="tpu_custom_call" | custom-call | flops 32212254720 | bytes 8388608 | tf_op jit(solution)/shard_map/lstm_grads/pallas_call | solution.py:226
  60.0 3.7 %all-to-all-start.1 = ((f32[4,72,1024]{2,1,0:T(8,128)}), f32[4,72,1024]{2,1,0:T(8,128)S(1)}, u32[]{:S(2)}, u32[]{:S(2)}) async-start(f32[4,72,1024]{2,1,0:T(8,128)} %add.118), calls=%async_computation.1 | async-start | bytes 2359296 | tf_op jit(solution)/shard_map/all_to_all | solution.py:433
  68.4 8.7 %collective-permute-done.9.mv3 = f32[40,1024]{1,0:T(8,128)S(1)} collective-permute-done((f32[40,1024]{1,0:T(8,128)S(1)}, f32[40,1024]{1,0:T(8,128)S(1)}, u32[]{:S(2)}, u32[]{:S(2)}) %collective-permute-start.9) | collective-permute-done | bytes 163872 | tf_op jit(solution)/shard_map/ppermute | solution.py:428
  77.1 5.0 %collective-permute-done.8.mv2 = f32[40,1024]{1,0:T(8,128)S(1)} collective-permute-done((f32[40,1024]{1,0:T(8,128)S(1)}, f32[40,1024]{1,0:T(8,128)S(1)}, u32[]{:S(2)}, u32[]{:S(2)}) %collective-permute-start.8) | collective-permute-done | bytes 163872 | tf_op jit(solution)/shard_map/ppermute | solution.py:428
  83.2 3.3 %first_adam.1 = (f32[72,1024]{1,0:T(8,128)}, f32[72,1024]{1,0:T(8,128)}, f32[72,1024]{1,0:T(8,128)}) custom-call(s32[3]{0:T(128)} %pad_add_fusion.refs_0_.who, f32[4,72,1024]{2,1,0:T(8,128)} %copy-done.1, f32[512,1024]{1,0:T(8,128)} %broadcast_select_fusion.refs_2_.w_ref, f32[1,1024]{1,0:T(1,128)} %broadcast_select_fusion.6.refs_3_.b_ref, ...), custom_call_target="tpu_custom_call" | custom-call | tf_op jit(solution)/shard_map/first_adam/pallas_call | solution.py:324
  86.4 1.9 collective-permute-start.10
  89.8 6.7 %collective-permute-done.10.refs_3_ = f32[72,1024]{1,0:T(8,128)S(1)} collective-permute-done((f32[72,1024]{1,0:T(8,128)}, f32[72,1024]{1,0:T(8,128)S(1)}, u32[]{:S(2)}, u32[]{:S(2)}) %collective-permute-start.10) | collective-permute-done | bytes 294944 | tf_op jit(solution)/shard_map/ppermute | solution.py:369
  97.3 5.9 %collective-permute-done.12.refs_5_ = f32[72,1024]{1,0:T(8,128)S(1)} collective-permute-done((f32[72,1024]{1,0:T(8,128)S(1)}, f32[72,1024]{1,0:T(8,128)S(1)}, u32[]{:S(2)}, u32[]{:S(2)}) %collective-permute-start.12) | collective-permute-done | bytes 294944 | tf_op jit(solution)/shard_map/ppermute | solution.py:369
  105.6 19.6 %lstm_grads.3 = (f32[4,72,1024]{2,1,0:T(8,128)}, f32[4,72,1024]{2,1,0:T(8,128)}) custom-call(s32[3]{0:T(128)} %pad_add_fusion.refs_0_.who, f32[4,19,8,256]{3,2,1,0:T(8,128)} %copy-done.4, f32[72,1024]{1,0:T(8,128)} %get-tuple-element.27.refs_2_.p_ref, f32[72,1024]{1,0:T(8,128)} %copy-done.26, f32[72,1024]{1,0:T(8,128)} %copy-done.27, f32[72,1024]{1,0:T(8,128)} %copy-done.28, ...), custom_call_target="tpu_custom_call" | custom-call | flops 32212254720 | bytes 8388608 | tf_op jit(solution)/shard_map/lstm_grads/pallas_call | solution.py:226
  125.4 2.9 %collective-permute-done.17 = f32[4,72,1024]{2,1,0:T(8,128)S(1)} collective-permute-done((f32[4,72,1024]{2,1,0:T(8,128)}, f32[4,72,1024]{2,1,0:T(8,128)S(1)}, u32[]{:S(2)}, u32[]{:S(2)}) %collective-permute-start.17) | collective-permute-done | bytes 1179680 | tf_op jit(solution)/shard_map/ppermute | solution.py:361
  129.7 19.3 %all_to_all.20.g_ref = f32[4,72,1024]{2,1,0:T(8,128)} all-to-all(f32[4,72,1024]{2,1,0:T(8,128)S(1)} %add.131), channel_id=1, replica_groups=mesh['k'=1,'c'=2,'q'=4,'r'=4] {'r'}, dimensions={0} | all-to-all | bytes 2359296 | tf_op jit(solution)/shard_map/all_to_all | solution.py:433
  149.1 2.7 %second_adam.1 = (f32[72,1024]{1,0:T(8,128)}, f32[4,40,1024]{2,1,0:T(8,128)}) custom-call(f32[4,72,1024]{2,1,0:T(8,128)} %all_to_all.20.g_ref, f32[72,1024]{1,0:T(8,128)} %get-tuple-element.27.refs_2_.p_ref, f32[72,1024]{1,0:T(8,128)} %get-tuple-element.30.m_ref, f32[72,1024]{1,0:T(8,128)} %get-tuple-element.31.v_ref), custom_call_target="tpu_custom_call" | custom-call | tf_op jit(solution)/shard_map/second_adam/pallas_call | solution.py:324
  151.7 4.7 %all-to-all-start.3 = ((f32[4,40,1024]{2,1,0:T(8,128)}), f32[4,40,1024]{2,1,0:T(8,128)S(1)}, u32[]{:S(2)}, u32[]{:S(2)}) async-start(f32[4,40,1024]{2,1,0:T(8,128)} %get-tuple-element.37), calls=%async_computation.3 | async-start | bytes 1310720 | tf_op jit(solution)/shard_map/all_to_all | solution.py:477
  156.4 3.8 %collective-permute-start.20 = (f32[72,1024]{1,0:T(8,128)}, f32[72,1024]{1,0:T(8,128)S(1)}, u32[]{:S(2)}, u32[]{:S(2)}) collective-permute-start(f32[72,1024]{1,0:T(8,128)} %get-tuple-element.32), channel_id=1, source_target_pairs={{0,12},{4,0},{8,4},{12,8},{1,13},{5,1},{9,5},{13,9},{2,14},{6,2},{... | collective-permute-start | bytes 884744 | tf_op jit(solution)/shard_map/ppermute | solution.py:455
  164.7 10.1 %collective-permute-done.20 = f32[72,1024]{1,0:T(8,128)S(1)} collective-permute-done((f32[72,1024]{1,0:T(8,128)}, f32[72,1024]{1,0:T(8,128)S(1)}, u32[]{:S(2)}, u32[]{:S(2)}) %collective-permute-start.20) | collective-permute-done | bytes 294944 | tf_op jit(solution)/shard_map/ppermute | solution.py:455
  174.8 23.4 %collective-permute-done.19 = f32[72,1024]{1,0:T(8,128)S(1)} collective-permute-done((f32[72,1024]{1,0:T(8,128)}, f32[72,1024]{1,0:T(8,128)S(1)}, u32[]{:S(2)}, u32[]{:S(2)}) %collective-permute-start.19) | collective-permute-done | bytes 294944 | tf_op jit(solution)/shard_map/ppermute | solution.py:455
  215.7 11.6 %collective-permute-done.25.refs_5_ = f32[2,72,1024]{2,1,0:T(8,128)S(1)} collective-permute-done((f32[2,72,1024]{2,1,0:T(8,128)S(1)}, f32[2,72,1024]{2,1,0:T(8,128)S(1)}, u32[]{:S(2)}, u32[]{:S(2)}) %collective-permute-start.25) | collective-permute-done | bytes 589856 | tf_op jit(solution)/shard_map/ppermute | solution.py:369
  230.8 7.1 %collective-permute-done.23.refs_3_ = f32[2,72,1024]{2,1,0:T(8,128)S(1)} collective-permute-done((f32[2,72,1024]{2,1,0:T(8,128)S(1)}, f32[2,72,1024]{2,1,0:T(8,128)S(1)}, u32[]{:S(2)}, u32[]{:S(2)}) %collective-permute-start.23) | collective-permute-done | bytes 589856 | tf_op jit(solution)/shard_map/ppermute | solution.py:369
  237.8 6.3 %collective-permute-done.27.refs_7_ = f32[2,72,1024]{2,1,0:T(8,128)S(1)} collective-permute-done((f32[2,72,1024]{2,1,0:T(8,128)S(1)}, f32[2,72,1024]{2,1,0:T(8,128)S(1)}, u32[]{:S(2)}, u32[]{:S(2)}) %collective-permute-start.27) | collective-permute-done | bytes 589856 | tf_op jit(solution)/shard_map/ppermute | solution.py:369
  245.0 4.7 %unpack.1 = (f32[2,512,1024]{2,1,0:T(8,128)}, f32[2,1024]{1,0:T(2,128)}, f32[2,256,128]{2,1,0:T(8,128)}, f32[2,128]{1,0:T(2,128)}) custom-call(s32[3]{0:T(128)} %pad_add_fusion.refs_0_.who, f32[2,72,1024]{2,1,0:T(8,128)} %copy-done.2, f32[2,72,1024]{2,1,0:T(8,128)} %copy-done.6, f32[2,72,1024]{2,1,0:T(8,128)} %copy-done.7, f32[2,72,1024]{2,1,0:T(8,128)} %copy-done.10, ...), custom_call_target="tpu_custom_call" | custom-call | tf_op jit(solution)/shard_map/unpack/pallas_call | solution.py:324
  (175 shorter events, 43.5 us)
Async XLA Ops:
  1.9 15.5 %collective-permute-start.4 = (f32[1,128]{1,0:T(1,128)}, f32[1,128]{1,0:T(1,128)}, u32[]{:S(2)}, u32[]{:S(2)}) collective-permute-start(f32[1,128]{1,0:T(1,128)} %constant_dynamic-slice_fusion.16), channel_id=1, source_target_pairs={{0,16},{16,0},{1,17},{17,1},{2,18},{18,2},{3,19},{19,3},{4,20},{20... | collective-permute-start | bytes 1544 | tf_op jit(solution)/shard_map/ppermute | solution.py:361
  5.6 14.3 %collective-permute-start.1 = (f32[512,1024]{1,0:T(8,128)}, f32[512,1024]{1,0:T(8,128)S(1)}, u32[]{:S(2)}, u32[]{:S(2)}) collective-permute-start(f32[512,1024]{1,0:T(8,128)} %dynamic-slice_bitcast_fusion), channel_id=1, source_target_pairs={{0,16},{16,0},{1,17},{17,1},{2,18},{18,2},{3,19},{19,3},{4,20},{20... | collective-permute-start | bytes 6291464 | tf_op jit(solution)/shard_map/ppermute | solution.py:361
  6.7 11.9 %collective-permute-start.2 = (f32[1,1024]{1,0:T(1,128)S(1)}, f32[1,1024]{1,0:T(1,128)S(1)}, u32[]{:S(2)}, u32[]{:S(2)}) collective-permute-start(f32[1,1024]{1,0:T(1,128)S(1)} %constant_dynamic-slice_fusion.17), channel_id=1, source_target_pairs={{0,16},{16,0},{1,17},{17,1},{2,18},{18,2},{3,19},{19,3},{4,20},{20... | collective-permute-start | bytes 12296 | tf_op jit(solution)/shard_map/ppermute | solution.py:361
  8.4 10.7 %collective-permute-start.3 = (f32[256,128]{1,0:T(8,128)}, f32[256,128]{1,0:T(8,128)}, u32[]{:S(2)}, u32[]{:S(2)}) collective-permute-start(f32[256,128]{1,0:T(8,128)} %dynamic-slice_bitcast_fusion.2), channel_id=1, source_target_pairs={{0,16},{16,0},{1,17},{17,1},{2,18},{18,2},{3,19},{19,3},{4,20},{20... | collective-permute-start | bytes 393224 | tf_op jit(solution)/shard_map/ppermute | solution.py:361
  11.3 23.1 %all-to-all-start = ((f32[4,19,8,256]{3,2,1,0:T(8,128)}), f32[4,19,8,256]{3,2,1,0:T(8,128)S(1)}, u32[]{:S(2)}, u32[]{:S(2)}) async-start(f32[4,19,8,256]{3,2,1,0:T(8,128)} %pad_maximum_fusion), calls=%async_computation | async-start | bytes 1245184 | tf_op jit(solution)/shard_map/all_to_all | solution.py:402
  60.0 22.1 %all-to-all-start.1 = ((f32[4,72,1024]{2,1,0:T(8,128)}), f32[4,72,1024]{2,1,0:T(8,128)S(1)}, u32[]{:S(2)}, u32[]{:S(2)}) async-start(f32[4,72,1024]{2,1,0:T(8,128)} %add.118), calls=%async_computation.1 | async-start | bytes 2359296 | tf_op jit(solution)/shard_map/all_to_all | solution.py:433
  66.3 10.8 %collective-permute-start.9 = (f32[40,1024]{1,0:T(8,128)S(1)}, f32[40,1024]{1,0:T(8,128)S(1)}, u32[]{:S(2)}, u32[]{:S(2)}) collective-permute-start(f32[40,1024]{1,0:T(8,128)S(1)} %get-tuple-element.54), channel_id=1, source_target_pairs={{0,12},{4,0},{8,4},{12,8},{1,13},{5,1},{9,5},{13,9},{2,14},{6,2},{... | collective-permute-start | bytes 491528 | tf_op jit(solution)/shard_map/ppermute | solution.py:428
  67.8 9.3 %collective-permute-start.7 = (f32[40,1024]{1,0:T(8,128)S(1)}, f32[40,1024]{1,0:T(8,128)S(1)}, u32[]{:S(2)}, u32[]{:S(2)}) collective-permute-start(f32[40,1024]{1,0:T(8,128)S(1)} %get-tuple-element.56), channel_id=1, source_target_pairs={{0,4},{4,8},{8,12},{12,0},{1,5},{5,9},{9,13},{13,1},{2,6},{6,10},{... | collective-permute-start | bytes 491528 | tf_op jit(solution)/shard_map/ppermute | solution.py:428
  68.4 13.8 %collective-permute-start.8 = (f32[40,1024]{1,0:T(8,128)S(1)}, f32[40,1024]{1,0:T(8,128)S(1)}, u32[]{:S(2)}, u32[]{:S(2)}) collective-permute-start(f32[40,1024]{1,0:T(8,128)S(1)} %get-tuple-element.57), channel_id=1, source_target_pairs={{0,8},{4,12},{8,0},{12,4},{1,9},{5,13},{9,1},{13,5},{2,10},{6,14},... | collective-permute-start | bytes 491528 | tf_op jit(solution)/shard_map/ppermute | solution.py:428
  86.4 10.1 %collective-permute-start.10 = (f32[72,1024]{1,0:T(8,128)}, f32[72,1024]{1,0:T(8,128)S(1)}, u32[]{:S(2)}, u32[]{:S(2)}) collective-permute-start(f32[72,1024]{1,0:T(8,128)} %get-tuple-element.27.refs_2_.p_ref), channel_id=1, source_target_pairs={{0,1},{1,0},{2,3},{3,2},{16,18},{17,19},{18,16},{19,17},{4,5},{5,4... | collective-permute-start | bytes 884744 | tf_op jit(solution)/shard_map/ppermute | solution.py:369
  88.4 8.9 %collective-permute-start.11 = (f32[72,1024]{1,0:T(8,128)}, f32[72,1024]{1,0:T(8,128)S(1)}, u32[]{:S(2)}, u32[]{:S(2)}) collective-permute-start(f32[72,1024]{1,0:T(8,128)} %get-tuple-element.27.refs_2_.p_ref), channel_id=1, source_target_pairs={{0,2},{1,3},{2,0},{3,1},{16,17},{17,16},{18,19},{19,18},{4,6},{5,7... | collective-permute-start | bytes 884744 | tf_op jit(solution)/shard_map/ppermute | solution.py:369
  96.5 6.7 %collective-permute-start.12 = (f32[72,1024]{1,0:T(8,128)S(1)}, f32[72,1024]{1,0:T(8,128)S(1)}, u32[]{:S(2)}, u32[]{:S(2)}) collective-permute-start(f32[72,1024]{1,0:T(8,128)S(1)} %collective-permute-done.10.refs_3_), channel_id=1, source_target_pairs={{0,2},{1,3},{2,0},{3,1},{16,17},{17,16},{18,19},{19,18},{4,6},{5,7... | collective-permute-start | bytes 884744 | tf_op jit(solution)/shard_map/ppermute | solution.py:369
  96.7 6.6 %collective-permute-start.14 = (f32[72,1024]{1,0:T(8,128)S(1)}, f32[72,1024]{1,0:T(8,128)S(1)}, u32[]{:S(2)}, u32[]{:S(2)}) collective-permute-start(f32[72,1024]{1,0:T(8,128)S(1)} %collective-permute-done.10.refs_3_), channel_id=1, source_target_pairs={{0,16},{16,0},{1,17},{17,1},{2,18},{18,2},{3,19},{19,3},{4,20},{20... | collective-permute-start | bytes 884744 | tf_op jit(solution)/shard_map/ppermute | solution.py:361
  151.7 56.9 %all-to-all-start.3 = ((f32[4,40,1024]{2,1,0:T(8,128)}), f32[4,40,1024]{2,1,0:T(8,128)S(1)}, u32[]{:S(2)}, u32[]{:S(2)}) async-start(f32[4,40,1024]{2,1,0:T(8,128)} %get-tuple-element.37), calls=%async_computation.3 | async-start | bytes 1310720 | tf_op jit(solution)/shard_map/all_to_all | solution.py:477
  156.4 18.3 %collective-permute-start.20 = (f32[72,1024]{1,0:T(8,128)}, f32[72,1024]{1,0:T(8,128)S(1)}, u32[]{:S(2)}, u32[]{:S(2)}) collective-permute-start(f32[72,1024]{1,0:T(8,128)} %get-tuple-element.32), channel_id=1, source_target_pairs={{0,12},{4,0},{8,4},{12,8},{1,13},{5,1},{9,5},{13,9},{2,14},{6,2},{... | collective-permute-start | bytes 884744 | tf_op jit(solution)/shard_map/ppermute | solution.py:455
  160.3 37.9 %collective-permute-start.19 = (f32[72,1024]{1,0:T(8,128)}, f32[72,1024]{1,0:T(8,128)S(1)}, u32[]{:S(2)}, u32[]{:S(2)}) collective-permute-start(f32[72,1024]{1,0:T(8,128)} %get-tuple-element.32), channel_id=1, source_target_pairs={{0,8},{4,12},{8,0},{12,4},{1,9},{5,13},{9,1},{13,5},{2,10},{6,14},... | collective-permute-start | bytes 884744 | tf_op jit(solution)/shard_map/ppermute | solution.py:455
  160.3 37.9 %collective-permute-start.18 = (f32[72,1024]{1,0:T(8,128)}, f32[72,1024]{1,0:T(8,128)S(1)}, u32[]{:S(2)}, u32[]{:S(2)}) collective-permute-start(f32[72,1024]{1,0:T(8,128)} %get-tuple-element.32), channel_id=1, source_target_pairs={{0,4},{4,8},{8,12},{12,0},{1,5},{5,9},{9,13},{13,1},{2,6},{6,10},{... | collective-permute-start | bytes 884744 | tf_op jit(solution)/shard_map/ppermute | solution.py:455
  199.4 10.4 %collective-permute-start.24 = (f32[2,72,1024]{2,1,0:T(8,128)S(1)}, f32[2,72,1024]{2,1,0:T(8,128)S(1)}, u32[]{:S(2)}, u32[]{:S(2)}) collective-permute-start(f32[2,72,1024]{2,1,0:T(8,128)S(1)} %pad_maximum_fusion.2), channel_id=1, source_target_pairs={{0,16},{16,0},{1,17},{17,1},{2,18},{18,2},{3,19},{19,3},{4,20},{20... | collective-permute-start | bytes 1769480 | tf_op jit(solution)/shard_map/ppermute | solution.py:361
  199.5 12.2 %collective-permute-start.21 = (f32[2,72,1024]{2,1,0:T(8,128)S(1)}, f32[2,72,1024]{2,1,0:T(8,128)S(1)}, u32[]{:S(2)}, u32[]{:S(2)}) collective-permute-start(f32[2,72,1024]{2,1,0:T(8,128)S(1)} %pad_maximum_fusion.1.refs_0_), channel_id=1, source_target_pairs={{0,1},{1,0},{2,3},{3,2},{16,18},{17,19},{18,16},{19,17},{4,5},{5,4... | collective-permute-start | bytes 1769480 | tf_op jit(solution)/shard_map/ppermute | solution.py:369
  209.0 21.8 %collective-permute-start.22 = (f32[2,72,1024]{2,1,0:T(8,128)S(1)}, f32[2,72,1024]{2,1,0:T(8,128)S(1)}, u32[]{:S(2)}, u32[]{:S(2)}) collective-permute-start(f32[2,72,1024]{2,1,0:T(8,128)S(1)} %pad_maximum_fusion.1.refs_0_), channel_id=1, source_target_pairs={{0,2},{1,3},{2,0},{3,1},{16,17},{17,16},{18,19},{19,18},{4,6},{5,7... | collective-permute-start | bytes 1769480 | tf_op jit(solution)/shard_map/ppermute | solution.py:369
  209.8 28.1 %collective-permute-start.26 = (f32[2,72,1024]{2,1,0:T(8,128)S(1)}, f32[2,72,1024]{2,1,0:T(8,128)S(1)}, u32[]{:S(2)}, u32[]{:S(2)}) collective-permute-start(f32[2,72,1024]{2,1,0:T(8,128)S(1)} %collective-permute-done.24.refs_4_), channel_id=1, source_target_pairs={{0,2},{1,3},{2,0},{3,1},{16,17},{17,16},{18,19},{19,18},{4,6},{5,7... | collective-permute-start | bytes 1769480 | tf_op jit(solution)/shard_map/ppermute | solution.py:369
  211.0 16.3 %collective-permute-start.25 = (f32[2,72,1024]{2,1,0:T(8,128)S(1)}, f32[2,72,1024]{2,1,0:T(8,128)S(1)}, u32[]{:S(2)}, u32[]{:S(2)}) collective-permute-start(f32[2,72,1024]{2,1,0:T(8,128)S(1)} %collective-permute-done.24.refs_4_), channel_id=1, source_target_pairs={{0,1},{1,0},{2,3},{3,2},{16,18},{17,19},{18,16},{19,17},{4,5},{5,4... | collective-permute-start | bytes 1769480 | tf_op jit(solution)/shard_map/ppermute | solution.py:369
  211.7 26.2 %collective-permute-start.23 = (f32[2,72,1024]{2,1,0:T(8,128)S(1)}, f32[2,72,1024]{2,1,0:T(8,128)S(1)}, u32[]{:S(2)}, u32[]{:S(2)}) collective-permute-start(f32[2,72,1024]{2,1,0:T(8,128)S(1)} %collective-permute-done.21.refs_1_), channel_id=1, source_target_pairs={{0,2},{1,3},{2,0},{3,1},{16,17},{17,16},{18,19},{19,18},{4,6},{5,7... | collective-permute-start | bytes 1769480 | tf_op jit(solution)/shard_map/ppermute | solution.py:369
  227.3 16.9 %collective-permute-start.27 = (f32[2,72,1024]{2,1,0:T(8,128)S(1)}, f32[2,72,1024]{2,1,0:T(8,128)S(1)}, u32[]{:S(2)}, u32[]{:S(2)}) collective-permute-start(f32[2,72,1024]{2,1,0:T(8,128)S(1)} %collective-permute-done.25.refs_5_), channel_id=1, source_target_pairs={{0,2},{1,3},{2,0},{3,1},{16,17},{17,16},{18,19},{19,18},{4,6},{5,7... | collective-permute-start | bytes 1769480 | tf_op jit(solution)/shard_map/ppermute | solution.py:369
  (41 other events, 377.7 us)

commit v2 on v1

v2 whole, which is shorter than its diff:
```python
import functools
import jax
import jax.numpy as jnp
import numpy as np
from jax import lax
from jax.experimental import pallas as pl
from jax.experimental.pallas import tpu as pltpu
from jax.sharding import Mesh, PartitionSpec as P

F32 = jnp.float32
BF16 = jnp.bfloat16
LOSS_SCALE = 1.0 / 256.0
QUAD = 4
NN = ((1,), (0,))
NT = ((1,), (1,))
TN = ((0,), (0,))
VMEM_LIMIT = 56 << 20
SMALL = pl.CostEstimate(flops=1, transcendentals=0, bytes_accessed=1)


class Either:
    def __init__(self, flag, a, b):
        self.flag, self.a, self.b = flag, a, b

    def __getitem__(self, at):
        return jnp.where(self.flag, self.a[at], self.b[at])


def split(x):
    hi = x.astype(BF16)
    return hi, (x - hi.astype(F32)).astype(BF16)


def mm(a, b, dims):
    return lax.dot_general(a, b, (dims, ((), ())), preferred_element_type=F32)


def dot3(a, b, dims):
    return mm(a[0], b[0], dims) + (mm(a[1], b[0], dims) + mm(a[0], b[1], dims))


def dot3_few(a, b, dims):
    n = a[0].shape[0]
    r = mm(jnp.concatenate([a[0], a[1]], 0), b[0], dims)
    return r[:n] + (r[n:] + mm(a[0], b[1], dims))


class Sizes:
    def __init__(self, R, rows, wide, hid, act):
        self.R, self.rows, self.wide, self.hid, self.act = R, rows, wide, hid, act
        D = QUAD * R
        self.B = rows // D
        self.half = self.B // 2
        self.W = QUAD * self.half
        self.h = hid // D // 2
        self.CH = self.W + 8
        self.b_each = wide // D
        self.hb_each = act // D
        self.bl = wide // 2


def own_bias(S, r):
    at = lax.broadcasted_iota(jnp.int32, (2, S.bl), 0) * S.bl + lax.broadcasted_iota(jnp.int32, (2, S.bl), 1)
    return ((at // S.b_each) & (S.R - 1)) == r


def own_head_bias(S, r):
    at = lax.broadcasted_iota(jnp.int32, (1, S.act), 1)
    return ((at // S.hb_each) & (S.R - 1)) == r


def grad_kernel(S, T, packed, *refs):
    who, x_refs = refs[0], refs[1 : 1 + QUAD]
    n_in = 2 * S.R if packed else 8
    w_in = refs[1 + QUAD : 1 + QUAD + n_in]
    refs = refs[1 + QUAD + n_in :]
    keep, send = refs[: S.R], refs[S.R : 2 * S.R]
    (xs, zx, gi, gf, gg, go, tc, cp, hs, dhh, lgs, dzh, dzl, whi, wlo, ws, whs, bs, hbs, sem) = refs[-20:]
    c, r = who[0], who[1]
    nb = x_refs[0].shape[1]
    IN = x_refs[0].shape[2]
    H = S.hid
    N = QUAD * nb
    rows_all = T * N
    R, B, half, W, h = S.R, S.B, S.half, S.W, S.h

    if packed:
        rel_of = bit_orders(R)
        bias = jnp.zeros((2, S.bl), F32)
        hbias = jnp.zeros((1, S.act), F32)
        for i in range(2 * R):
            mine = i < R
            ref = w_in[i]
            hc = c if mine else 1 - c
            rel = jnp.where(hc == 0, rel_of[0][i % R], rel_of[1][i % R])
            src = r ^ rel
            for z in range(QUAD):
                at = pl.multiple_of((z * R + src) * B + hc * half, half)
                ws[pl.ds(at, half), :] = ref[z * half : (z + 1) * half, :]
                at = pl.multiple_of(((z * R + src) * 2 + hc) * h, h)
                whs[pl.ds(at, h), :] = ref[W : W + h, z * S.act : (z + 1) * S.act]
            bias += jnp.where(hc == 0, ref[W : W + 2, S.bl :], 0.0)
            hbias += jnp.where(hc == 0, ref[W + 2 : W + 3, S.bl : S.bl + S.act], 0.0)
        bs[:, 0 : S.bl] = bias[0:1]
        bs[:, S.bl :] = bias[1:2]
        hbs[...] = hbias
        w_ref, b_ref, wh_ref, hb_ref = ws, bs, whs, hbs
    else:
        mine, at = (who[2] >> 1) == c, who[2] & 1

        @pl.when(mine)
        def _():
            pltpu.make_async_copy(w_in[0].at[at], ws, sem).start()

        @pl.when(jnp.logical_not(mine))
        def _():
            pltpu.make_async_copy(w_in[4].at[at], ws, sem).start()

        for i, ref in ((1, bs), (2, whs), (3, hbs)):
            ref[...] = jnp.where(mine, w_in[i][at], w_in[4 + i][at])
        w_ref, b_ref, wh_ref, hb_ref = ws, bs, whs, hbs

    for z in range(QUAD):
        xs[:, z] = x_refs[z][0:T]
    xv = split(xs[...].reshape(rows_all, IN))
    if not packed:
        pltpu.make_async_copy(w_in[0].at[0], ws, sem).wait()
    hi, lo = split(w_ref[...])
    whi[...] = hi
    wlo[...] = lo
    if not packed:
        own = refs[2 * S.R]
        for z in range(QUAD):
            own[z * half : (z + 1) * half, :] = w_ref[pl.ds(pl.multiple_of((z * R + r) * B + c * half, half), half), :]
        own[W:, :] = jnp.zeros((8, S.wide), F32)
        for z in range(QUAD):
            at = pl.multiple_of(((z * R + r) * 2 + c) * h, h)
            own[W : W + h, z * S.act : (z + 1) * S.act] = wh_ref[pl.ds(at, h), :]
        b2 = b_ref[...]
        b2 = jnp.concatenate([b2[:, 0 : S.bl], b2[:, S.bl :]], axis=0)
        own[W : W + 2, S.bl :] = jnp.where(own_bias(S, r), b2, 0.0)
        own[W + 2 : W + 3, S.bl : S.bl + S.act] = jnp.where(own_head_bias(S, r), hb_ref[...], 0.0)

    zx[...] = dot3(xv, (whi[0:IN], wlo[0:IN]), NN) + b_ref[...]
    h0, c0, aux = (jnp.concatenate([x[T + i] for x in x_refs], axis=0) for i in range(3))

    def forward(t, carry):
        hv, cv = carry
        at = pl.ds(pl.multiple_of(t * N, N), N)
        hs[at, :] = hv
        cp[at, :] = cv
        z = zx[at, :] + dot3_few(split(hv), (whi[IN:], wlo[IN:]), NN)
        i = jax.nn.sigmoid(z[:, 0:H])
        f = jax.nn.sigmoid(z[:, H : 2 * H])
        g = jnp.tanh(z[:, 2 * H : 3 * H])
        o = jax.nn.sigmoid(z[:, 3 * H :])
        cv = f * cv + i * g
        th = jnp.tanh(cv)
        gi[at, :] = i
        gf[at, :] = f
        gg[at, :] = g
        go[at, :] = o
        tc[at, :] = th
        return o * th, cv

    hv, _ = lax.fori_loop(0, T, forward, (h0, c0))
    hs[rows_all : rows_all + N, :] = hv

    hh = split(hs[N : rows_all + N, :])
    whp = split(wh_ref[...])
    lgs[...] = dot3(hh, whp, NN) + hb_ref[...]
    lane = lax.broadcasted_iota(jnp.int32, (N, S.act), 1).astype(F32)
    for t in range(T):
        lg = lgs[t * N : (t + 1) * N, :]
        e = jnp.exp(lg - jnp.max(lg, axis=1, keepdims=True))
        p = e / jnp.sum(e, axis=1, keepdims=True)
        hot = jnp.where(lane == aux[:, IN // 2 + t : IN // 2 + t + 1], 1.0, 0.0)
        lgs[t * N : (t + 1) * N, :] = (aux[:, t : t + 1] * LOSS_SCALE) * (p - hot)
    dl = lgs[...]
    d_hb = jnp.sum(dl, axis=0, keepdims=True)
    dls = split(dl)
    whs[...] = dot3(hh, dls, TN)
    dhh[...] = dot3(dls, whp, NT)

    def backward(k, carry):
        rec, dc = carry
        t = T - 1 - k
        at = pl.ds(pl.multiple_of(t * N, N), N)
        i, f, g, o, th = gi[at, :], gf[at, :], gg[at, :], go[at, :], tc[at, :]
        dh = dhh[at, :] + rec
        dc = dc + dh * o * (1.0 - th * th)
        dz = jnp.concatenate(
            [
                dc * g * (i * (1.0 - i)),
                dc * cp[at, :] * (f * (1.0 - f)),
                dc * i * (1.0 - g * g),
                dh * th * (o * (1.0 - o)),
            ],
            axis=1,
        )
        zh, zl = split(dz)
        dzh[at, :] = zh
        dzl[at, :] = zl
        zx[at, :] = dz
        return dot3_few((zh, zl), (whi[IN:], wlo[IN:]), NT), dc * f

    zero = jnp.zeros((N, H), F32)
    lax.fori_loop(0, T, backward, (zero, zero))
    d_b = jnp.sum(zx[...], axis=0, keepdims=True)

    dz = (dzh[...], dzl[...])
    span = R * B
    for z in range(QUAD):
        lo_row = z * span
        if lo_row < IN:
            left = (xv[0][:, lo_row : lo_row + span], xv[1][:, lo_row : lo_row + span])
        else:
            left = split(hs[0:rows_all, lo_row - IN : lo_row - IN + span])
        ws[lo_row : lo_row + span, :] = dot3(left, dz, TN)
    d_b2 = jnp.concatenate([d_b[:, 0 : S.bl], d_b[:, S.bl :]], axis=0)
    for rel in range(R):
        column = r ^ rel
        d_b_own = jnp.where(own_bias(S, column), d_b2, 0.0)
        d_hb_own = jnp.where(own_head_bias(S, column), d_hb, 0.0)
        for ref, side in ((keep[rel], c), (send[rel], 1 - c)):
            for z in range(QUAD):
                at = pl.multiple_of((z * R + column) * B + side * half, half)
                ref[z * half : (z + 1) * half, :] = ws[pl.ds(at, half), :]
            ref[W:, :] = jnp.zeros((8, S.wide), F32)
            ref[W : W + 2, S.bl :] = d_b_own
            ref[W + 2 : W + 3, S.bl : S.bl + S.act] = d_hb_own
            for z in range(QUAD):
                at = pl.multiple_of(((z * R + column) * 2 + side) * h, h)
                ref[W : W + h, z * S.act : (z + 1) * S.act] = whs[pl.ds(at, h), :]


def bit_orders(R):
    bits = [1 << s for s in range(R.bit_length() - 1)]
    orders = []
    for order in (bits, bits[::-1]):
        rels = [0]
        for b in order:
            rels += [x ^ b for x in rels]
        orders.append(rels)
    return orders


def grads_call(S, T, packed, who, x, weights):
    nb, IN = x[0].shape[1], x[0].shape[2]
    N = QUAD * nb
    rows = T * N
    V = pltpu.VMEM
    chunk = jax.ShapeDtypeStruct((S.CH, S.wide), F32)
    gate = V((rows, S.hid), F32)
    wide16 = V((rows, S.wide), BF16)
    w16 = V((S.rows, S.wide), BF16)
    n_in, n_out = len(weights), 2 * S.R + (0 if packed else 1)
    flops = 2 * rows * S.wide * (S.rows + S.rows + S.hid) * 3
    return pl.pallas_call(
        functools.partial(grad_kernel, S, T, packed),
        out_shape=[chunk] * n_out,
        in_specs=[pl.BlockSpec(memory_space=pltpu.SMEM)]
        + [pl.BlockSpec(memory_space=pltpu.VMEM)] * QUAD
        + [pl.BlockSpec(memory_space=pl.ANY if not packed and i % 4 == 0 else pltpu.VMEM) for i in range(n_in)],
        out_specs=[pl.BlockSpec(memory_space=pltpu.VMEM)] * n_out,
        scratch_shapes=[
            V((T, QUAD, nb, IN), F32),
            V((rows, S.wide), F32),
            gate, gate, gate, gate, gate, gate,
            V((rows + N, S.hid), F32),
            gate,
            V((rows, S.act), F32),
            wide16, wide16, w16, w16,
            V((S.rows, S.wide), F32),
            V((S.hid, S.act), F32),
            V((1, S.wide), F32),
            V((1, S.act), F32),
            pltpu.SemaphoreType.DMA,
        ],
        compiler_params=pltpu.CompilerParams(vmem_limit_bytes=VMEM_LIMIT),
        cost_estimate=pl.CostEstimate(flops=flops * 8, transcendentals=rows * S.hid * 5, bytes_accessed=8 << 20),
        name="lstm_grads",
    )(who, *x, *weights)


def adam(p, m, v, g):
    m = 0.9 * m + 0.1 * g
    v = 0.999 * v + 0.001 * g * g
    return p - 0.01 * m / (jnp.sqrt(v) + 1e-08), m, v


def total(parts):
    g = parts[0][...]
    for part in parts[1:]:
        g = g + part[...]
    return g


def put_gradient_blocks(S, q, g, outs):
    W, half, h = S.W, S.half, S.h
    for s, out in enumerate(outs):
        z = (q + s) & (QUAD - 1)
        out[0:half, :] = g[pl.ds(pl.multiple_of(z * half, half), half), :]
        out[half:, :] = g[W:, :]
        out[half : half + h, 0 : S.act] = g[W : W + h, pl.ds(pl.multiple_of(z * S.act, S.act), S.act)]


def first_adam_kernel(S, who, *refs):
    g_refs, p_ref, moments = refs[: S.R + 1], refs[S.R + 1], refs[S.R + 2 : S.R + 2 + QUAD]
    p_out, m_out, v_out = refs[S.R + 2 + QUAD : S.R + 5 + QUAD]
    g_outs, g_ref = refs[S.R + 5 + QUAD : -1], refs[-1]
    q = who[2]
    W, half, h, B = S.W, S.half, S.h, S.B
    g = total(g_refs)
    g_ref[...] = g
    put_gradient_blocks(S, q, g_ref, g_outs)
    mb = jnp.zeros((2, S.bl), F32)
    vb, mhb, vhb = mb, jnp.zeros((1, S.act), F32), jnp.zeros((1, S.act), F32)
    m_out[W:, :] = jnp.zeros((8, S.wide), F32)
    v_out[W:, :] = jnp.zeros((8, S.wide), F32)
    for s in range(QUAD):
        z = (q - s) & (QUAD - 1)
        ref = moments[s]
        at = pl.ds(pl.multiple_of(z * half, half), half)
        m_out[at, :] = ref[0:half, :]
        v_out[at, :] = ref[half:B, :]
        lanes = pl.ds(pl.multiple_of(z * S.act, S.act), S.act)
        m_out[W : W + h, lanes] = ref[B : B + h, 0 : S.act]
        v_out[W : W + h, lanes] = ref[B : B + h, S.act : 2 * S.act]
        mb = mb + ref[B : B + 2, S.bl :]
        vb = vb + ref[B + 2 : B + 4, S.bl :]
        mhb = mhb + ref[B + 4 : B + 5, S.bl : S.bl + S.act]
        vhb = vhb + ref[B + 5 : B + 6, S.bl : S.bl + S.act]
    m_out[W : W + 2, S.bl :] = mb
    v_out[W : W + 2, S.bl :] = vb
    m_out[W + 2 : W + 3, S.bl : S.bl + S.act] = mhb
    v_out[W + 2 : W + 3, S.bl : S.bl + S.act] = vhb
    p_out[...], m_out[...], v_out[...] = adam(p_ref[...], m_out[...], v_out[...], g)


def second_adam_kernel(S, who, *refs):
    g_refs, (p_ref, m_ref, v_ref, p_out), g_outs, g_ref = refs[: S.R + 1], refs[S.R + 1 : S.R + 5], refs[S.R + 5 : -1], refs[-1]
    g = total(g_refs)
    g_ref[...] = g
    p_out[...] = adam(p_ref[...], m_ref[...], v_ref[...], g)[0]
    put_gradient_blocks(S, who[2], g_ref, g_outs)


def moments_kernel(S, who, here, there, *refs):
    first, second, out = refs[:QUAD], refs[QUAD : 2 * QUAD], refs[2 * QUAD]
    c, q = who[0], who[2]
    half, h, B = S.half, S.h, S.B
    for s in range(QUAD):
        j = (q - s) & (QUAD - 1)
        blocks = Either((j >> 1) == c, here, there)

        def put(m_at, m_lanes, v_at, v_lanes, g_at, g_lanes):
            m, v = blocks[j & 1, m_at, m_lanes], blocks[j & 1, v_at, v_lanes]
            for ref in (first[s], second[s]):
                _, m, v = adam(0.0, m, v, ref[g_at, g_lanes])
            out[j, m_at, m_lanes] = m
            out[j, v_at, v_lanes] = v

        out[j, B:, :] = jnp.zeros((8, S.wide), F32)
        every, tail, one = slice(None), slice(S.bl, None), slice(S.bl, S.bl + S.act)
        put(slice(0, half), every, slice(half, B), every, slice(0, half), every)
        put(slice(B, B + h), slice(0, S.act), slice(B, B + h), slice(S.act, 2 * S.act), slice(half, half + h), slice(0, S.act))
        put(slice(B, B + 2), tail, slice(B + 2, B + 4), tail, slice(half, half + 2), tail)
        put(slice(B + 4, B + 5), one, slice(B + 5, B + 6), one, slice(half + 2, half + 3), one)


def spread(x, width, d):
    each = x.shape[1]
    lane = lax.broadcasted_iota(jnp.int32, (x.shape[0], width), 1) - d * each
    out = jnp.zeros((x.shape[0], width), F32)
    for i in range(each):
        out = jnp.where(lane == i, x[:, i : i + 1], out)
    return out


def pack_moments_kernel(S, who, m, v, mh, vh, mb, vb, mhb, vhb, here, there):
    c, d = who[0], who[2] * S.R + who[1]
    L, B, half, h = m.shape[0], S.B, S.half, S.h
    biases = [spread(x[...], S.wide, d) for x in (mb, vb)]
    head_biases = [spread(x[...], S.act, d) for x in (mhb, vhb)]
    for l in range(L):
        for ref, side in ((here, c), (there, 1 - c)):
            at = pl.ds(pl.multiple_of(side * half, half), half)
            ref[l, 0:half, :] = m[l, at, :]
            ref[l, half:B, :] = v[l, at, :]
            ref[l, B:, :] = jnp.zeros((8, S.wide), F32)
            at = pl.ds(pl.multiple_of(side * h, h), h)
            ref[l, B : B + h, 0 : S.act] = mh[l, at, :]
            ref[l, B : B + h, S.act : 2 * S.act] = vh[l, at, :]
            for i in range(2):
                ref[l, B + 2 * i : B + 2 * i + 1, S.bl :] = biases[i][l : l + 1, 0 : S.bl]
                ref[l, B + 2 * i + 1 : B + 2 * i + 2, S.bl :] = biases[i][l : l + 1, S.bl :]
                ref[l, B + 4 + i : B + 5 + i, S.bl : S.bl + S.act] = head_biases[i][l : l + 1]


def route_kernel(who, here, there, *outs):
    c, q = who[0], who[2]
    for s, out in enumerate(outs):
        j = (q + s) & (QUAD - 1)
        out[...] = Either((j >> 1) == c, here, there)[j & 1]


def choose_kernel(slots, n, L, who, *refs):
    pieces, out, sem = refs[: slots * n], refs[slots * n], refs[slots * n + 1]
    for i in range(n):
        for l in range(L):
            for j in range(slots):

                @pl.when(who[3 + L + l] == j)
                def _():
                    pltpu.make_async_copy(pieces[j * n + i], out.at[i, l], sem.at[i, l]).start()

    for i in range(n):
        for l in range(L):
            pltpu.make_async_copy(pieces[i], out.at[i, l], sem.at[i, l]).wait()


def pack_kernel(T, who, x_ref, h_ref, c_ref, adv_ref, act_ref, here, there):
    L, _, _, IN = x_ref.shape
    nb = here.shape[2]
    for l in range(L):
        for ref, side in ((here, who[0]), (there, 1 - who[0])):
            at = pl.ds(pl.multiple_of(side * nb, nb), nb)
            for t in range(T):
                ref[l, t] = x_ref[l, at, t, :]
            ref[l, T] = h_ref[l, at, :]
            ref[l, T + 1] = c_ref[l, at, :]
            ref[l, T + 2] = jnp.zeros((nb, IN), F32)
            ref[l, T + 2, :, 0:T] = adv_ref[l, at, :]
            ref[l, T + 2, :, IN // 2 : IN // 2 + T] = act_ref[l, at, :].astype(F32)


def vmem_call(fn, name, out_shape, smem, *args, scratch=(), cost=SMALL, space=pltpu.VMEM, out_specs=None):
    specs = [pl.BlockSpec(memory_space=pltpu.SMEM)] * smem
    specs += [pl.BlockSpec(memory_space=space)] * (len(args) - smem)
    return pl.pallas_call(
        fn,
        out_shape=out_shape,
        in_specs=specs,
        out_specs=out_specs or jax.tree.map(lambda _: pl.BlockSpec(memory_space=space), out_shape),
        scratch_shapes=scratch,
        cost_estimate=cost,
        compiler_params=pltpu.CompilerParams(vmem_limit_bytes=VMEM_LIMIT),
        name=name,
    )(*args)


def unpack_kernel(S, L, groups, slots, who, *refs):
    R, B, half, W, h = S.R, S.B, S.half, S.W, S.h
    own, other = refs[: slots * R], refs[slots * R : slots * R + len(groups)]
    w_out, b_out, wh_out, hb_out, rest, sem, rest_sem = refs[slots * R + len(groups) :]
    c, r = who[0], who[1]
    rel_of = bit_orders(R)

    def source(i, hc):
        return r ^ jnp.where(hc == 0, rel_of[0][i], rel_of[1][i])

    def copies(piece, l, i, o):
        hc = c if o == 0 else 1 - c
        src = source(i, hc)
        for z in range(QUAD):
            at = pl.multiple_of((z * R + src) * B + hc * half, half)
            yield pltpu.make_async_copy(piece.at[pl.ds(z * half, half)], w_out.at[l, pl.ds(at, half)], sem.at[l, i, o, z])
        yield pltpu.make_async_copy(piece.at[pl.ds(W, 8)], rest.at[l, i, o], rest_sem.at[l, i, o])

    cases = []
    for g, columns in enumerate(groups):
        for at, i in enumerate(columns):
            for l in range(L):
                cases.append((other[g].at[at, l], l, i, 1))
    for l in range(L):
        for i in range(R):
            for j in range(slots):

                @pl.when(who[3 + l] == j)
                def _():
                    for copy in copies(own[j * R + i], l, i, 0):
                        copy.start()

    for case in cases:
        for copy in copies(*case):
            copy.start()
    waits = [list(copies(*case)) for case in cases]
    waits += [list(copies(own[i], l, i, 0)) for l in range(L) for i in range(R)]
    for group in waits:
        group[-1].wait()
    for l in range(L):
        bias = jnp.zeros((2, S.bl), F32)
        hbias = jnp.zeros((1, S.act), F32)
        for i in range(R):
            for o in range(2):
                hc = c if o == 0 else 1 - c
                src = source(i, hc)
                for z in range(QUAD):
                    at = pl.multiple_of(((z * R + src) * 2 + hc) * h, h)
                    wh_out[l, pl.ds(at, h), :] = rest[l, i, o, 0:h, z * S.act : (z + 1) * S.act]
            bias = bias + rest[l, i, 0, 0:2, S.bl :]
            hbias = hbias + rest[l, i, 0, 2:3, S.bl : S.bl + S.act]
        b_out[l : l + 1, 0 : S.bl] = bias[0:1]
        b_out[l : l + 1, S.bl :] = bias[1:2]
        hb_out[l : l + 1, :] = hbias
    for group in waits:
        for copy in group[:-1]:
            copy.wait()


def swap_cores(x):
    return lax.ppermute(x, "c", [(0, 1), (1, 0)])


def next_column(R, x, bits, i):
    up, down = bits[i], bits[-1 - i]
    return lax.ppermute(x, ("c", "r"), [(j, j ^ up) for j in range(R)] + [(R + j, R + (j ^ down)) for j in range(R)])


def gather_columns(R, x):
    bits = [1 << i for i in range(R.bit_length() - 1)]
    held = [x]
    for i in range(len(bits)):
        held += [next_column(R, y, bits, i) for y in held]
    return held


def along(x, pairs):
    return lax.ppermute(x, "q", pairs)


OUTER = [(0, 1), (1, 0), (2, 3), (3, 2)]
INNER = [(1, 2), (2, 1)]
OUTWARD = [(1, 0), (2, 3)]


def send_blocks(blocks):
    return blocks[:1] + [
        lax.ppermute(blocks[s], "q", [(i, (i + s) % QUAD) for i in range(QUAD)]) for s in range(1, QUAD)
    ]


def pick(options, index):
    out = options[-1]
    for i in range(len(options) - 2, -1, -1):
        out = jnp.where(index == i, options[i], out)
    return out


def local(K, R, features, actions, advantages, h_start, c_start, w_lstm, b_lstm, w_head, head_bias,
          m_lstm, m_bias, m_head, m_head_bias, v_lstm, v_bias, v_head, v_head_bias, winners, exploit_flags):
    L, n, T, IN = features.shape
    S = Sizes(R, w_lstm.shape[1], w_lstm.shape[2], w_head.shape[1], w_head.shape[2])
    k, c, q, r = (lax.axis_index(a).astype(jnp.int32) for a in "kcqr")
    D = QUAD * R
    bits = [1 << i for i in range(R.bit_length() - 1)]

    who = jnp.stack([c, r, q])

    part = jax.ShapeDtypeStruct((L, T + 3, n // 2, IN), F32)
    here, there = vmem_call(
        functools.partial(pack_kernel, T), "pack", (part, part), 1, who, features, h_start, c_start, advantages, actions
    )
    there = swap_cores(there)
    there, w_lstm = lax.optimization_barrier((there, w_lstm))
    weights = [w_lstm, b_lstm.reshape(L, 1, -1), w_head, head_bias.reshape(L, 1, -1)]
    weights += [swap_cores(w) for w in weights]
    message = jax.ShapeDtypeStruct(part.shape[1:], F32)
    outgoing = vmem_call(route_kernel, "route", [message] * QUAD, 1, who, here, there)
    x = send_blocks(list(outgoing))
    *weights, m_lstm, v_lstm, winners = lax.optimization_barrier((*weights, m_lstm, v_lstm, winners))

    slot_of = np.array([[0, 1, 2, 3], [1, 0, 2, 3], [3, 2, 0, 1], [3, 2, 1, 0]], np.int32)
    everyone = jnp.arange(winners.shape[0], dtype=jnp.int32)
    agents = 2 * k * L + np.tile(np.arange(L), 2) + L * jnp.where(np.arange(2 * L) < L, c, 1 - c)
    source = jnp.where(exploit_flags == 1, winners, everyone)
    source = jnp.sum(jnp.where(everyone[None] == agents[:, None], source[None], 0), axis=1)
    slot = jnp.sum(jnp.where(jnp.arange(QUAD)[:, None] == q, slot_of, 0), axis=0)
    slot = jnp.sum(jnp.where((source[:, None] & (QUAD - 1)) == np.arange(QUAD), slot[None], 0), axis=1)
    places = slot if K == 1 else jnp.arange(2 * L, dtype=jnp.int32)
    whose = jnp.concatenate([who, places.astype(jnp.int32), source.astype(jnp.int32)])

    part = jax.ShapeDtypeStruct((L, S.B + 8, S.wide), F32)
    m_here, m_there = vmem_call(
        functools.partial(pack_moments_kernel, S), "pack_moments", (part, part), 1,
        who, m_lstm, v_lstm, m_head, v_head, m_bias, v_bias, m_head_bias, v_head_bias,
    )

    m_there = swap_cores(m_there)
    message = jax.ShapeDtypeStruct(part.shape[1:], F32)
    outgoing = vmem_call(route_kernel, "route_moments", [message] * QUAD, 1, who, m_here, m_there)
    *both, whose = lax.optimization_barrier((*x, *weights, *outgoing, whose))
    x, weights, outgoing = both[:QUAD], both[QUAD:-QUAD], both[-QUAD:]

    chunk = jax.ShapeDtypeStruct((S.CH, S.wide), F32)
    block = [jax.ShapeDtypeStruct((S.half + 8, S.wide), F32)] * QUAD

    def reduced(keep, send, later):
        parts = {}
        for rel in range(R - 1, 0, -1):
            other = swap_cores(send[rel])
            if rel == R - 1:
                other, *later = lax.optimization_barrier((other, *later))
            parts[rel] = lax.ppermute(keep[rel] + other, "r", [(j, j ^ rel) for j in range(R)])
        return [keep[0], swap_cores(send[0])] + [parts[rel] for rel in range(1, R)], send_blocks(later)

    *g, p = grads_call(S, T, False, who, x, weights)
    g, moments = reduced(g[:R], g[R:], outgoing)
    p, m, v, *g = vmem_call(
        functools.partial(first_adam_kernel, S), "first_adam", [chunk] * 3 + block, 1,
        who, *g, p, *moments, scratch=[pltpu.VMEM((S.CH, S.wide), F32)],
    )
    held = gather_columns(R, p)
    held += [swap_cores(a) for a in held]
    g_out = g
    g = grads_call(S, T, True, who, x, held)
    g, g_first = reduced(g[:R], g[R:], g_out)
    p, *g_out = vmem_call(functools.partial(second_adam_kernel, S), "second_adam", [chunk] + block, 1, who, *g, p, m, v,
                           scratch=[pltpu.VMEM((S.CH, S.wide), F32)])

    outer, inner = [p], [p]
    steps = [
        lambda: [along(p, OUTER), along(p, INNER)],
        lambda: [along(inner[1], OUTWARD), along(outer[1], INNER)],
        lambda: [along(inner[2], OUTWARD)],
    ]
    middle = (q == 1) | (q == 2)
    arrivals = [
        lambda: p,
        lambda: outer[1],
        lambda: jnp.where(middle, inner[1], outer[2]),
        lambda: jnp.where(middle, inner[2], outer[3]),
    ]

    own = []
    starts = [QUAD - 1] * QUAD if K > 1 else list(range(QUAD))
    for t in range(starts[-1] + len(bits)):
        if K == 1 and t < QUAD:
            own.append([arrivals[t]()])
        if K > 1 and t == QUAD - 1:
            groups = lax.all_gather(jnp.stack([f() for f in arrivals]), "k").reshape(K * QUAD, S.CH, S.wide)
            for i in range(2 * L):
                at = (source[i] // QUAD) * QUAD + slot[i]
                own.append([lax.dynamic_index_in_dim(groups, at, 0, keepdims=False)])
        moved = steps[t]() if t < QUAD - 1 else []
        n_steps = len(moved)
        for j, held in enumerate(own):
            if 0 <= t - starts[j] < len(bits):
                moved += [next_column(R, x, bits, t - starts[j]) for x in held]
        if t == QUAD - 2:
            g_second = send_blocks(g_out)
            moved += g_second
        if t == QUAD - 1:
            mv = vmem_call(
                functools.partial(moments_kernel, S), "moments", jax.ShapeDtypeStruct((QUAD, S.B + 8, S.wide), F32), 1,
                who, m_here, m_there, *g_first, *g_second,
            )
            if K > 1:
                mv = lax.all_gather(mv, "k").reshape(K * QUAD, S.B + 8, S.wide)
            chosen = [
                jnp.stack([lax.dynamic_index_in_dim(mv, source[side * L + l].astype(jnp.uint32), 0, keepdims=False) for l in range(L)])
                for side in range(2)
            ]
            moved += chosen
        before = [x for held in own for x in held]
        if t < starts[-1] + len(bits) - 1:
            moved = list(lax.optimization_barrier((*moved, *before, *g_out)))
            before = moved[len(moved) - len(before) - QUAD : len(moved) - QUAD]
            g_out = moved[len(moved) - QUAD :]
        for j, held in enumerate(own):
            own[j] = [before.pop(0) for _ in held]
        for path, _ in zip((outer, inner), range(n_steps)):
            path.append(moved.pop(0))
        for j, held in enumerate(own):
            if 0 <= t - starts[j] < len(bits):
                held += [moved.pop(0) for _ in list(held)]
        if t == QUAD - 2:
            g_second = [moved.pop(0) for _ in range(QUAD)]
        if t == QUAD - 1:
            chosen = [moved.pop(0) for _ in range(2)]
            mv_there = swap_cores(chosen[1])

    f = lambda *dims: jax.ShapeDtypeStruct(dims, F32)
    columns = [list(range(R // 2)), list(range(R // 2, R))]
    vm = pl.BlockSpec(memory_space=pltpu.VMEM)
    other = []
    for group in columns:
        pieces = [held[i] for held in own for i in group]
        out = vmem_call(
            functools.partial(choose_kernel, len(own), len(group), L), "choose", f(len(group), L, S.CH, S.wide), 1,
            whose, *pieces, space=pl.ANY, out_specs=vm, scratch=[pltpu.SemaphoreType.DMA((len(group), L))],
        )
        other.append(swap_cores(out))
    new_w, new_b, new_wh, new_hb = vmem_call(
        functools.partial(unpack_kernel, S, L, columns, len(own)), "unpack",
        (f(L, S.rows, S.wide), f(L, S.wide), f(L, S.hid, S.act), f(L, S.act)), 1,
        whose, *[a for held in own for a in held], *other, space=pl.ANY,
        out_specs=(vm, vm, vm, vm),
        scratch=[pltpu.VMEM((L, R, 2, 8, S.wide), F32), pltpu.SemaphoreType.DMA((L, R, 2, QUAD)),
                 pltpu.SemaphoreType.DMA((L, R, 2))],
    )

    here, there = chosen[0], mv_there
    lo, hi = jnp.where(c == 0, here, there), jnp.where(c == 0, there, here)
    B, half, h = S.B, S.half, S.h
    d = (q * R + r).astype(jnp.uint32)
    out = []
    for i in range(2):
        rows = jnp.concatenate([a[:, i * half : (i + 1) * half] for a in (lo, hi)], axis=1)
        bias = lo[:, B + 2 * i : B + 2 * i + 2, S.bl :].reshape(L, S.wide)
        head = jnp.concatenate([a[:, B : B + h, i * S.act : (i + 1) * S.act] for a in (lo, hi)], axis=1)
        hb = lo[:, B + 4 + i, S.bl : S.bl + S.act]
        out += [
            rows,
            lax.dynamic_slice_in_dim(bias, d * S.b_each, S.b_each, 1),
            head,
            lax.dynamic_slice_in_dim(hb, d * S.hb_each, S.hb_each, 1),
        ]
    return (new_w, new_b, new_wh, new_hb, *out)


def solution(mesh):
    M, D = mesh.shape["member"], mesh.shape["dp"]
    K, R = M // 2, D // QUAD
    inner = Mesh(mesh.devices.reshape(K, 2, QUAD, R), ("k", "c", "q", "r"))
    member, dp = ("k", "c"), ("q", "r")
    full = [P(member, None, None), P(member, None), P(member, None, None), P(member, None)]
    rows = [P(member, dp, None), P(member, dp), P(member, dp, None), P(member, dp)]
    seqs = [P(member, dp, None, None)] + [P(member, dp, None)] * 4
    return jax.shard_map(
        functools.partial(local, K, R),
        mesh=inner,
        in_specs=(*seqs, *full, *rows, *rows, P(), P()),
        out_specs=(*full, *rows, *rows),
        check_vma=False,
    )
```

time: 251 us -> 229 us (0.912)
  waiting for transfers between devices: 103 us -> 71.6 us
  starting transfers between devices: 34.2 us -> 60.5 us
  blocking collectives: 19.3 us -> 0 us
  Pallas kernels: 49.7 us -> 68.5 us
  between operations: 11.5 us -> 4.14 us
  other arithmetic: 15.6 us -> 9.36 us
  local copies, waits for them, and re-layouts: 16.4 us -> 13.7 us
    ppermute x15 -> x38, starting transfers between devices: 16.7 us -> 56 us  [the longest x12 26.5 us: send_blocks(): lax.ppermute(blocks[s], 'q', [(i, (i + s) % QUAD) for i in range(QUAD)])]
    all_to_all x1 -> x0, blocking collectives: 19.3 us -> none  [reduced(): return lax.all_to_all(keep + swap_cores(send), 'r', 0, 0, tiled=True)]
    pallas_call x5 -> x12, Pallas kernels: 49.7 us -> 68.5 us  [the longest x2 40.1 us: grads_call(): pl.pallas_call(functools.partial(grad_kernel, S, T, packed), out_shape=[c...]
    ppermute x15 -> x38, waiting for transfers between devices: 84.8 us -> 66.2 us  [the longest x15 24.5 us: next_column(): lax.ppermute(x, ('c', 'r'), [(j, j ^ up) for j in range(R)] + [(R + j, R...]
    all_to_all x3 -> x0, starting transfers between devices: 14.5 us -> none  [the longest x1 6.02 us: local(): x = lax.all_to_all(x, 'q', 0, 0, tiled=True)]
    all_to_all x3 -> x0, waiting for transfers between devices: 11.3 us -> none  [the longest x1 11.3 us: local(): x = lax.all_to_all(x, 'q', 0, 0, tiled=True)]
    squeeze x5 -> x0, local copies, waits for them, and re-layouts: 5.95 us -> none  [the longest x4 5.93 us: local(): lax.dynamic_index_in_dim(x, q & 1, 0, keepdims=False)]
    select_n x8 -> x3, other arithmetic: 5.9 us -> 0.08 us  [the longest x1 0.05 us: local(): jnp.where(middle, inner[2], outer[3])]
  transfers between devices with their start and end apart: 32 -> 59, of which waited for: 14 -> 23; matrix products, arithmetic and copies ran while one was open for 10% -> 6% of each run, Pallas kernels for 0% -> 6%
where the time goes in v2:
time: 229 us; the launch traced here: 228 us
  waiting for transfers between devices  71.6 us (31%)
  Pallas kernels  68.5 us (30%)
  starting transfers between devices  60.5 us (26%)
  local copies, waits for them, and re-layouts  13.7 us (6%)
  other arithmetic  9.36 us (4%)
  between operations  4.14 us (2%)
    pallas_call x2, Pallas kernels, grads_call(): pl.pallas_call(functools.partial(grad_kernel, S, T, packed), out_shape=[c...  40.1 us
    pallas_call x10, Pallas kernels, vmem_call(): pl.pallas_call(fn, out_shape=out_shape, in_specs=specs, out_specs=out_spe...  28.4 us
    ppermute x12, starting transfers between devices, send_blocks(): lax.ppermute(blocks[s], 'q', [(i, (i + s) % QUAD) for i in range(QUAD)])  26.5 us
    ppermute x15, waiting for transfers between devices, next_column(): lax.ppermute(x, ('c', 'r'), [(j, j ^ up) for j in range(R)] + [(R + j, R...  24.5 us
    ppermute x12, waiting for transfers between devices, send_blocks(): lax.ppermute(blocks[s], 'q', [(i, (i + s) % QUAD) for i in range(QUAD)])  20.1 us
    ppermute x15, starting transfers between devices, next_column(): lax.ppermute(x, ('c', 'r'), [(j, j ^ up) for j in range(R)] + [(R + j, R...  14.8 us
    ppermute x6, waiting for transfers between devices, reduced(): lax.ppermute(keep[rel] + other, 'r', [(j, j ^ rel) for j in range(R)])  14.6 us
    unnamed x121, local copies, waits for them, and re-layouts  7.97 us
  transfers between devices with their start and end apart: 59, of which 23 were waited for; matrix products, arithmetic and copies ran while one was open for 6% of the time, Pallas kernels for 6%

profile of v2, /device:TPU:0, one launch (start us, length us, event | category | flops | bytes accessed | tf_op | source)
XLA Modules:
  0.0 227.8 jit_solution(1756896792805327644)
XLA Ops:
  10.5 2.9 %collective-permute-start.1 = (f32[19,8,256]{2,1,0:T(8,128)}, f32[19,8,256]{2,1,0:T(8,128)S(1)}, u32[]{:S(2)}, u32[]{:S(2)}) collective-permute-start(f32[19,8,256]{2,1,0:T(8,128)} %get-tuple-element.152), channel_id=1, source_target_pairs={{0,4},{4,8},{8,12},{12,0},{1,5},{5,9},{9,13},{13,1},{2,6},{6,10},{... | collective-permute-start | bytes 466952 | tf_op jit(solution)/shard_map/ppermute | solution.py:540
  27.5 20.6 %lstm_grads.2 = (f32[72,1024]{1,0:T(8,128)}, f32[72,1024]{1,0:T(8,128)}, f32[72,1024]{1,0:T(8,128)}, f32[72,1024]{1,0:T(8,128)}, f32[72,1024]{1,0:T(8,128)}, /*i...) custom-call(s32[3]{0:T(128)} %pad_add_fusion.who.refs_0_, ...), custom_call_target="tpu_custom_call" | custom-call | flops 32212254720 | bytes 8388608 | tf_op jit(solution)/shard_map/lstm_grads/pallas_call | solution.py:259
  50.0 3.7 %collective-permute-start.16 = (f32[40,1024]{1,0:T(8,128)S(1)}, f32[40,1024]{1,0:T(8,128)S(1)}, u32[]{:S(2)}, u32[]{:S(2)}) collective-permute-start(f32[40,1024]{1,0:T(8,128)S(1)} %copy-done.48), channel_id=1, source_target_pairs={{0,4},{4,8},{8,12},{12,0},{1,5},{5,9},{9,13},{13,1},{2,6},{6,10},{... | collective-permute-start | bytes 491528 | tf_op jit(solution)/shard_map/ppermute | solution.py:540
  62.6 6.8 %collective-permute-done.17.refs_8_ = f32[40,1024]{1,0:T(8,128)S(1)} collective-permute-done((f32[40,1024]{1,0:T(8,128)S(1)}, f32[40,1024]{1,0:T(8,128)S(1)}, u32[]{:S(2)}, u32[]{:S(2)}) %collective-permute-start.17) | collective-permute-done | bytes 163872 | tf_op jit(solution)/shard_map/ppermute | solution.py:540
  73.1 2.9 %first_adam.1 = (f32[72,1024]{1,0:T(8,128)}, f32[72,1024]{1,0:T(8,128)}, f32[72,1024]{1,0:T(8,128)}, f32[24,1024]{1,0:T(8,128)}, f32[24,1024]{1,0:T(8,128)}, /*index=5*/f32[24,1024]{1,0:T(8,128)}, f32[24,1024]{1,0:T(8,128)}) custom-call(s32[3]{0:T(128)} %pad_add_fusion.who.refs_0_, f32[72,1024]{1,0:T(8,128)} %get-tuple-element.186.refs_0_, ...), custom_call_target="tpu_custom_call" | custom-call | flops 1 | bytes 1 | tf_op jit(solution)/shard_map/first_adam/pallas_call | solution.py:441
  78.1 8.1 %collective-permute-done.19.refs_6_ = f32[72,1024]{1,0:T(8,128)S(1)} collective-permute-done((f32[72,1024]{1,0:T(8,128)}, f32[72,1024]{1,0:T(8,128)S(1)}, u32[]{:S(2)}, u32[]{:S(2)}) %collective-permute-start.19) | collective-permute-done | bytes 294944 | tf_op jit(solution)/shard_map/ppermute | solution.py:518
  86.7 6.1 %collective-permute-done.21.refs_8_ = f32[72,1024]{1,0:T(8,128)S(1)} collective-permute-done((f32[72,1024]{1,0:T(8,128)S(1)}, f32[72,1024]{1,0:T(8,128)S(1)}, u32[]{:S(2)}, u32[]{:S(2)}) %collective-permute-start.21) | collective-permute-done | bytes 294944 | tf_op jit(solution)/shard_map/ppermute | solution.py:518
  95.2 19.5 %lstm_grads.3 = (f32[72,1024]{1,0:T(8,128)}, f32[72,1024]{1,0:T(8,128)}, f32[72,1024]{1,0:T(8,128)}, f32[72,1024]{1,0:T(8,128)}, f32[72,1024]{1,0:T(8,128)}, /*i...) custom-call(s32[3]{0:T(128)} %pad_add_fusion.who.refs_0_, f32[19,8,256]{2,1,0:T(8,128)} %get-tuple-element.174.refs_1_, ...), custom_call_target="tpu_custom_call" | custom-call | flops 32212254720 | bytes 8388608 | tf_op jit(solution)/shard_map/lstm_grads/pallas_call | solution.py:259
  119.3 3.0 %collective-permute-start.32 = (f32[72,1024]{1,0:T(8,128)S(1)}, f32[72,1024]{1,0:T(8,128)S(1)}, u32[]{:S(2)}, u32[]{:S(2)}) collective-permute-start(f32[72,1024]{1,0:T(8,128)S(1)} %add.32), channel_id=1, source_target_pairs={{0,3},{1,2},{2,1},{3,0},{4,7},{5,6},{6,5},{7,4},{8,11},{9,10},{10,... | collective-permute-start | bytes 884744 | tf_op jit(solution)/shard_map/ppermute | solution.py:605
  122.3 5.2 %collective-permute-done.28.refs_2_ = f32[72,1024]{1,0:T(8,128)S(1)} collective-permute-done((f32[72,1024]{1,0:T(8,128)S(1)}, f32[72,1024]{1,0:T(8,128)S(1)}, u32[]{:S(2)}, u32[]{:S(2)}) %collective-permute-start.28) | collective-permute-done | bytes 294944 | tf_op jit(solution)/shard_map/ppermute | solution.py:605
  127.5 6.8 %collective-permute-done.30.refs_3_ = f32[72,1024]{1,0:T(8,128)S(1)} collective-permute-done((f32[72,1024]{1,0:T(8,128)S(1)}, f32[72,1024]{1,0:T(8,128)S(1)}, u32[]{:S(2)}, u32[]{:S(2)}) %collective-permute-start.30) | collective-permute-done | bytes 294944 | tf_op jit(solution)/shard_map/ppermute | solution.py:605
  135.2 2.7 %second_adam.1 = (f32[72,1024]{1,0:T(8,128)}, f32[24,1024]{1,0:T(8,128)}, f32[24,1024]{1,0:T(8,128)}, f32[24,1024]{1,0:T(8,128)}, f32[24,1024]{1,0:T(8,128)}) custom-call(s32[3]{0:T(128)} %pad_add_fusion.who.refs_0_, f32[72,1024]{1,0:T(8,128)} %get-tuple-element.205.refs_0_, f32[72,1024]{1,0:T(8,128)} %copy-done.18, f32[72,1024]{1,0:T(8,128)} %copy-done.19, ...), custom_call_target="tpu_custom_call" | custom-call | flops 1 | bytes 1 | tf_op jit(solution)/shard_map/second_adam/pallas_call | solution.py:441
  140.0 3.5 %collective-permute-start.33 = (f32[72,1024]{1,0:T(8,128)}, f32[72,1024]{1,0:T(8,128)S(1)}, u32[]{:S(2)}, u32[]{:S(2)}) collective-permute-start(f32[72,1024]{1,0:T(8,128)} %get-tuple-element.264.refs_0_), channel_id=1, source_target_pairs={{0,4},{4,0},{8,12},{12,8},{1,5},{5,1},{9,13},{13,9},{2,6},{6,2},{1... | collective-permute-start | bytes 884744 | tf_op jit(solution)/shard_map/ppermute | solution.py:530
  144.8 3.9 %collective-permute-done.33.refs_2_.refs_4_ = f32[72,1024]{1,0:T(8,128)S(1)} collective-permute-done((f32[72,1024]{1,0:T(8,128)}, f32[72,1024]{1,0:T(8,128)S(1)}, u32[]{:S(2)}, u32[]{:S(2)}) %collective-permute-start.33) | collective-permute-done | bytes 294944 | tf_op jit(solution)/shard_map/ppermute | solution.py:530
  154.1 3.2 %collective-permute-done.36 = f32[72,1024]{1,0:T(8,128)S(1)} collective-permute-done((f32[72,1024]{1,0:T(8,128)S(1)}, f32[72,1024]{1,0:T(8,128)S(1)}, u32[]{:S(2)}, u32[]{:S(2)}) %collective-permute-start.36) | collective-permute-done | bytes 294944 | tf_op jit(solution)/shard_map/ppermute | solution.py:530
  158.4 3.2 %collective-permute-done.39.refs_1_.refs_3_ = f32[72,1024]{1,0:T(8,128)S(1)} collective-permute-done((f32[72,1024]{1,0:T(8,128)S(1)}, f32[72,1024]{1,0:T(8,128)S(1)}, u32[]{:S(2)}, u32[]{:S(2)}) %collective-permute-start.39) | collective-permute-done | bytes 294944 | tf_op jit(solution)/shard_map/ppermute | solution.py:518
  161.5 4.2 %collective-permute-start.45 = (f32[24,1024]{1,0:T(8,128)}, f32[24,1024]{1,0:T(8,128)S(1)}, u32[]{:S(2)}, u32[]{:S(2)}) collective-permute-start(f32[24,1024]{1,0:T(8,128)} %get-tuple-element.238), channel_id=1, source_target_pairs={{0,4},{4,8},{8,12},{12,0},{1,5},{5,9},{9,13},{13,1},{2,6},{6,10},{... | collective-permute-start | bytes 294920 | tf_op jit(solution)/shard_map/ppermute | solution.py:540
  171.8 5.2 %collective-permute-done.46.refs_6_ = f32[24,1024]{1,0:T(8,128)S(1)} collective-permute-done((f32[24,1024]{1,0:T(8,128)}, f32[24,1024]{1,0:T(8,128)S(1)}, u32[]{:S(2)}, u32[]{:S(2)}) %collective-permute-start.46) | collective-permute-done | bytes 98336 | tf_op jit(solution)/shard_map/ppermute | solution.py:540
  177.0 3.1 %collective-permute-start.47 = (f32[24,1024]{1,0:T(8,128)}, f32[24,1024]{1,0:T(8,128)S(1)}, u32[]{:S(2)}, u32[]{:S(2)}) collective-permute-start(f32[24,1024]{1,0:T(8,128)} %get-tuple-element.240), channel_id=1, source_target_pairs={{0,12},{4,0},{8,4},{12,8},{1,13},{5,1},{9,5},{13,9},{2,14},{6,2},{... | collective-permute-start | bytes 294920 | tf_op jit(solution)/shard_map/ppermute | solution.py:540
  180.1 4.7 %collective-permute-done.47.refs_7_ = f32[24,1024]{1,0:T(8,128)S(1)} collective-permute-done((f32[24,1024]{1,0:T(8,128)}, f32[24,1024]{1,0:T(8,128)S(1)}, u32[]{:S(2)}, u32[]{:S(2)}) %collective-permute-start.47) | collective-permute-done | bytes 98336 | tf_op jit(solution)/shard_map/ppermute | solution.py:540
  202.6 2.9 %choose.2 = f32[2,2,72,1024]{3,2,1,0:T(8,128)} custom-call(s32[11]{0:T(128)} %concatenate.16.who, f32[72,1024]{1,0:T(8,128)} %get-tuple-element.264.refs_0_, f32[72,1024]{1,0:T(8,128)} %copy-done.3, f32[72,1024]{1,0:T(8,128)} %copy-done.4, f32[72,1024]{1,0:T(8,128)} %copy-done.7, f32[72,1024]{1,0:T(8,128)} %copy-done, f32[72,1024]{1,0:T(8,128)} %copy-done.8, ...), custom_call_target="tpu_custom_call" | custom-call | flops 1 | bytes 1 | tf_op jit(solution)/shard_map/choose/pallas_call | solution.py:441
  207.2 3.2 %collective-permute-done.55.refs_7_.refs_15_ = f32[72,1024]{1,0:T(8,128)S(1)} collective-permute-done((f32[72,1024]{1,0:T(8,128)}, f32[72,1024]{1,0:T(8,128)S(1)}, u32[]{:S(2)}, u32[]{:S(2)}) %collective-permute-start.55) | collective-permute-done | bytes 294944 | tf_op jit(solution)/shard_map/ppermute | solution.py:518
  211.2 3.0 %choose.3 = f32[2,2,72,1024]{3,2,1,0:T(8,128)} custom-call(s32[11]{0:T(128)} %concatenate.16.who, f32[72,1024]{1,0:T(8,128)} %copy-done.5, f32[72,1024]{1,0:T(8,128)} %copy-done.6, f32[72,1024]{1,0:T(8,128)} %copy-done.9, f32[72,1024]{1,0:T(8,128)} %copy-done.10, f32[72,1024]{1,0:T(8,128)} %copy-done.11, f32[72,1024]{1,0:T(8,128)} %copy-done.12, ...), custom_call_target="tpu_custom_call" | custom-call | flops 1 | bytes 1 | tf_op jit(solution)/shard_map/choose/pallas_call | solution.py:441
  221.7 6.0 %unpack.1 = (f32[2,512,1024]{2,1,0:T(8,128)}, f32[2,1024]{1,0:T(2,128)}, f32[2,256,128]{2,1,0:T(8,128)}, f32[2,128]{1,0:T(2,128)}) custom-call(s32[11]{0:T(128)} %concatenate.16.who, f32[72,1024]{1,0:T(8,128)} %get-tuple-element.264.refs_0_, f32[72,1024]{1,0:T(8,128)} %copy-done.3, f32[72,1024]{1,0:T(8,128)} %copy-done.5, f32[72,1024]{1,0:T(8,128)} %copy-done.6, ...), custom_call_target="tpu_custom_call" | custom-call | flops 1 | bytes 1 | tf_op jit(solution)/shard_map/unpack/pallas_call | solution.py:441
  (262 shorter events, 89.3 us)
Async XLA Ops:
  5.3 12.1 %collective-permute-start.4 = (f32[2,512,1024]{2,1,0:T(8,128)}, f32[2,512,1024]{2,1,0:T(8,128)}, u32[]{:S(2)}, u32[]{:S(2)}) collective-permute-start(f32[2,512,1024]{2,1,0:T(8,128)} %refs_5_), channel_id=1, source_target_pairs={{0,16},{16,0},{1,17},{17,1},{2,18},{18,2},{3,19},{19,3},{4,20},{20... | collective-permute-start | bytes 12582920 | tf_op jit(solution)/shard_map/ppermute | solution.py:513
  6.9 10.5 %collective-permute-start.6 = (f32[2,256,128]{2,1,0:T(8,128)}, f32[2,256,128]{2,1,0:T(8,128)S(1)}, u32[]{:S(2)}, u32[]{:S(2)}) collective-permute-start(f32[2,256,128]{2,1,0:T(8,128)} %refs_7_), channel_id=1, source_target_pairs={{0,16},{16,0},{1,17},{17,1},{2,18},{18,2},{3,19},{19,3},{4,20},{20... | collective-permute-start | bytes 786440 | tf_op jit(solution)/shard_map/ppermute | solution.py:513
  10.5 13.9 %collective-permute-start.1 = (f32[19,8,256]{2,1,0:T(8,128)}, f32[19,8,256]{2,1,0:T(8,128)S(1)}, u32[]{:S(2)}, u32[]{:S(2)}) collective-permute-start(f32[19,8,256]{2,1,0:T(8,128)} %get-tuple-element.152), channel_id=1, source_target_pairs={{0,4},{4,8},{8,12},{12,0},{1,5},{5,9},{9,13},{13,1},{2,6},{6,10},{... | collective-permute-start | bytes 466952 | tf_op jit(solution)/shard_map/ppermute | solution.py:540
  13.5 13.3 %collective-permute-start.2 = (f32[19,8,256]{2,1,0:T(8,128)}, f32[19,8,256]{2,1,0:T(8,128)S(1)}, u32[]{:S(2)}, u32[]{:S(2)}) collective-permute-start(f32[19,8,256]{2,1,0:T(8,128)} %get-tuple-element.153), channel_id=1, source_target_pairs={{0,8},{4,12},{8,0},{12,4},{1,9},{5,13},{9,1},{13,5},{2,10},{6,14},... | collective-permute-start | bytes 466952 | tf_op jit(solution)/shard_map/ppermute | solution.py:540
  16.1 10.7 %collective-permute-start.3 = (f32[19,8,256]{2,1,0:T(8,128)}, f32[19,8,256]{2,1,0:T(8,128)S(1)}, u32[]{:S(2)}, u32[]{:S(2)}) collective-permute-start(f32[19,8,256]{2,1,0:T(8,128)} %get-tuple-element.154), channel_id=1, source_target_pairs={{0,12},{4,0},{8,4},{12,8},{1,13},{5,1},{9,5},{13,9},{2,14},{6,2},{... | collective-permute-start | bytes 466952 | tf_op jit(solution)/shard_map/ppermute | solution.py:540
  48.8 10.7 %collective-permute-start.9 = (f32[72,1024]{1,0:T(8,128)}, f32[72,1024]{1,0:T(8,128)S(1)}, u32[]{:S(2)}, u32[]{:S(2)}) collective-permute-start(f32[72,1024]{1,0:T(8,128)} %get-tuple-element.187), channel_id=1, source_target_pairs={{0,16},{16,0},{1,17},{17,1},{2,18},{18,2},{3,19},{19,3},{4,20},{20... | collective-permute-start | bytes 884744 | tf_op jit(solution)/shard_map/ppermute | solution.py:513
  50.0 11.3 %collective-permute-start.16 = (f32[40,1024]{1,0:T(8,128)S(1)}, f32[40,1024]{1,0:T(8,128)S(1)}, u32[]{:S(2)}, u32[]{:S(2)}) collective-permute-start(f32[40,1024]{1,0:T(8,128)S(1)} %copy-done.48), channel_id=1, source_target_pairs={{0,4},{4,8},{8,12},{12,0},{1,5},{5,9},{9,13},{13,1},{2,6},{6,10},{... | collective-permute-start | bytes 491528 | tf_op jit(solution)/shard_map/ppermute | solution.py:540
  54.8 14.9 %collective-permute-start.11 = (f32[72,1024]{1,0:T(8,128)S(1)}, f32[72,1024]{1,0:T(8,128)S(1)}, u32[]{:S(2)}, u32[]{:S(2)}) collective-permute-start(f32[72,1024]{1,0:T(8,128)S(1)} %add.27), channel_id=1, source_target_pairs={{0,1},{1,0},{2,3},{3,2},{4,5},{5,4},{6,7},{7,6},{8,9},{9,8},{10,11... | collective-permute-start | bytes 884744 | tf_op jit(solution)/shard_map/ppermute | solution.py:605
  57.4 14.9 %collective-permute-start.13 = (f32[72,1024]{1,0:T(8,128)S(1)}, f32[72,1024]{1,0:T(8,128)S(1)}, u32[]{:S(2)}, u32[]{:S(2)}) collective-permute-start(f32[72,1024]{1,0:T(8,128)S(1)} %add.28), channel_id=1, source_target_pairs={{0,2},{1,3},{2,0},{3,1},{4,6},{5,7},{6,4},{7,5},{8,10},{9,11},{10,... | collective-permute-start | bytes 884744 | tf_op jit(solution)/shard_map/ppermute | solution.py:605
  59.0 13.3 %collective-permute-start.15 = (f32[72,1024]{1,0:T(8,128)S(1)}, f32[72,1024]{1,0:T(8,128)S(1)}, u32[]{:S(2)}, u32[]{:S(2)}) collective-permute-start(f32[72,1024]{1,0:T(8,128)S(1)} %add.29), channel_id=1, source_target_pairs={{0,3},{1,2},{2,1},{3,0},{4,7},{5,6},{6,5},{7,4},{8,11},{9,10},{10,... | collective-permute-start | bytes 884744 | tf_op jit(solution)/shard_map/ppermute | solution.py:605
  76.0 10.2 %collective-permute-start.19 = (f32[72,1024]{1,0:T(8,128)}, f32[72,1024]{1,0:T(8,128)S(1)}, u32[]{:S(2)}, u32[]{:S(2)}) collective-permute-start(f32[72,1024]{1,0:T(8,128)} %get-tuple-element.204.refs_5_), channel_id=1, source_target_pairs={{0,1},{1,0},{2,3},{3,2},{16,18},{17,19},{18,16},{19,17},{4,5},{5,4... | collective-permute-start | bytes 884744 | tf_op jit(solution)/shard_map/ppermute | solution.py:518
  76.6 10.1 %collective-permute-start.20 = (f32[72,1024]{1,0:T(8,128)}, f32[72,1024]{1,0:T(8,128)S(1)}, u32[]{:S(2)}, u32[]{:S(2)}) collective-permute-start(f32[72,1024]{1,0:T(8,128)} %get-tuple-element.204.refs_5_), channel_id=1, source_target_pairs={{0,2},{1,3},{2,0},{3,1},{16,17},{17,16},{18,19},{19,18},{4,6},{5,7... | collective-permute-start | bytes 884744 | tf_op jit(solution)/shard_map/ppermute | solution.py:518
  117.6 9.9 %collective-permute-start.28 = (f32[72,1024]{1,0:T(8,128)S(1)}, f32[72,1024]{1,0:T(8,128)S(1)}, u32[]{:S(2)}, u32[]{:S(2)}) collective-permute-start(f32[72,1024]{1,0:T(8,128)S(1)} %add.30), channel_id=1, source_target_pairs={{0,1},{1,0},{2,3},{3,2},{4,5},{5,4},{6,7},{7,6},{8,9},{9,8},{10,11... | collective-permute-start | bytes 884744 | tf_op jit(solution)/shard_map/ppermute | solution.py:605
  119.2 15.2 %collective-permute-start.30 = (f32[72,1024]{1,0:T(8,128)S(1)}, f32[72,1024]{1,0:T(8,128)S(1)}, u32[]{:S(2)}, u32[]{:S(2)}) collective-permute-start(f32[72,1024]{1,0:T(8,128)S(1)} %add.31), channel_id=1, source_target_pairs={{0,2},{1,3},{2,0},{3,1},{4,6},{5,7},{6,4},{7,5},{8,10},{9,11},{10,... | collective-permute-start | bytes 884744 | tf_op jit(solution)/shard_map/ppermute | solution.py:605
  119.3 15.0 %collective-permute-start.32 = (f32[72,1024]{1,0:T(8,128)S(1)}, f32[72,1024]{1,0:T(8,128)S(1)}, u32[]{:S(2)}, u32[]{:S(2)}) collective-permute-start(f32[72,1024]{1,0:T(8,128)S(1)} %add.32), channel_id=1, source_target_pairs={{0,3},{1,2},{2,1},{3,0},{4,7},{5,6},{6,5},{7,4},{8,11},{9,10},{10,... | collective-permute-start | bytes 884744 | tf_op jit(solution)/shard_map/ppermute | solution.py:605
  151.3 10.2 %collective-permute-start.39 = (f32[72,1024]{1,0:T(8,128)S(1)}, f32[72,1024]{1,0:T(8,128)S(1)}, u32[]{:S(2)}, u32[]{:S(2)}) collective-permute-start(f32[72,1024]{1,0:T(8,128)S(1)} %collective-permute-done.35.refs_1_), channel_id=1, source_target_pairs={{0,2},{1,3},{2,0},{3,1},{16,17},{17,16},{18,19},{19,18},{4,6},{5,7... | collective-permute-start | bytes 884744 | tf_op jit(solution)/shard_map/ppermute | solution.py:518
  165.7 20.1 %collective-permute-start.44 = (f32[72,1024]{1,0:T(8,128)S(1)}, f32[72,1024]{1,0:T(8,128)S(1)}, u32[]{:S(2)}, u32[]{:S(2)}) collective-permute-start(f32[72,1024]{1,0:T(8,128)S(1)} %broadcast_select_fusion.3.refs_4_.refs_8_), channel_id=1, source_target_pairs={{0,1},{1,0},{2,3},{3,2},{16,18},{17,19},{18,16},{19,17},{4,5},{5,4... | collective-permute-start | bytes 884744 | tf_op jit(solution)/shard_map/ppermute | solution.py:518
  166.9 20.5 %collective-permute-start.41 = (f32[72,1024]{1,0:T(8,128)S(1)}, f32[72,1024]{1,0:T(8,128)S(1)}, u32[]{:S(2)}, u32[]{:S(2)}) collective-permute-start(f32[72,1024]{1,0:T(8,128)S(1)} %collective-permute-done.37), channel_id=1, source_target_pairs={{4,0},{8,12},{5,1},{9,13},{6,2},{10,14},{7,3},{11,15},{20,16},{24,... | collective-permute-start | bytes 884744 | tf_op jit(solution)/shard_map/ppermute | solution.py:530
  168.2 20.6 %collective-permute-start.42 = (f32[72,1024]{1,0:T(8,128)S(1)}, f32[72,1024]{1,0:T(8,128)S(1)}, u32[]{:S(2)}, u32[]{:S(2)}) collective-permute-start(f32[72,1024]{1,0:T(8,128)S(1)} %collective-permute-done.33.refs_2_.refs_4_), channel_id=1, source_target_pairs={{0,2},{1,3},{2,0},{3,1},{16,17},{17,16},{18,19},{19,18},{4,6},{5,7... | collective-permute-start | bytes 884744 | tf_op jit(solution)/shard_map/ppermute | solution.py:518
  168.8 20.0 %collective-permute-start.43 = (f32[72,1024]{1,0:T(8,128)S(1)}, f32[72,1024]{1,0:T(8,128)S(1)}, u32[]{:S(2)}, u32[]{:S(2)}) collective-permute-start(f32[72,1024]{1,0:T(8,128)S(1)} %collective-permute-done.40.refs_3_.refs_5_), channel_id=1, source_target_pairs={{0,2},{1,3},{2,0},{3,1},{16,17},{17,16},{18,19},{19,18},{4,6},{5,7... | collective-permute-start | bytes 884744 | tf_op jit(solution)/shard_map/ppermute | solution.py:518
  188.9 11.5 %collective-permute-start.50 = (f32[72,1024]{1,0:T(8,128)S(1)}, f32[72,1024]{1,0:T(8,128)}, u32[]{:S(2)}, u32[]{:S(2)}) collective-permute-start(f32[72,1024]{1,0:T(8,128)S(1)} %broadcast_select_fusion.2.refs_6_.refs_12_), channel_id=1, source_target_pairs={{0,1},{1,0},{2,3},{3,2},{16,18},{17,19},{18,16},{19,17},{4,5},{5,4... | collective-permute-start | bytes 884744 | tf_op jit(solution)/shard_map/ppermute | solution.py:518
  190.1 10.3 %collective-permute-start.48 = (f32[72,1024]{1,0:T(8,128)S(1)}, f32[72,1024]{1,0:T(8,128)S(1)}, u32[]{:S(2)}, u32[]{:S(2)}) collective-permute-start(f32[72,1024]{1,0:T(8,128)S(1)} %broadcast_select_fusion.3.refs_4_.refs_8_), channel_id=1, source_target_pairs={{0,2},{1,3},{2,0},{3,1},{16,17},{17,16},{18,19},{19,18},{4,6},{5,7... | collective-permute-start | bytes 884744 | tf_op jit(solution)/shard_map/ppermute | solution.py:518
  200.4 13.9 %collective-permute-start.58 = (f32[2,40,1024]{2,1,0:T(8,128)S(1)}, f32[2,40,1024]{2,1,0:T(8,128)S(1)}, u32[]{:S(2)}, u32[]{:S(2)}) collective-permute-start(f32[2,40,1024]{2,1,0:T(8,128)S(1)} %get-tuple-element.283), channel_id=1, source_target_pairs={{0,16},{16,0},{1,17},{17,1},{2,18},{18,2},{3,19},{19,3},{4,20},{20... | collective-permute-start | bytes 983048 | tf_op jit(solution)/shard_map/ppermute | solution.py:513
  205.5 14.1 %collective-permute-start.56 = (f32[2,2,72,1024]{3,2,1,0:T(8,128)}, f32[2,2,72,1024]{3,2,1,0:T(8,128)S(1)}, u32[]{:S(2)}, u32[]{:S(2)}) collective-permute-start(f32[2,2,72,1024]{3,2,1,0:T(8,128)} %choose.2), channel_id=1, source_target_pairs={{0,16},{16,0},{1,17},{17,1},{2,18},{18,2},{3,19},{19,3},{4,20},{20... | collective-permute-start | bytes 3538952 | tf_op jit(solution)/shard_map/ppermute | solution.py:513
  (94 other events, 978.2 us)
